TPU v7x, 32 devices: a whole 2x2x4 slice. The times are simulated.
32 devices in a mesh: seq: 16 (over z, x, core), vocab: 2 (over y).
Axes of the slice: x: 2, y: 2, z: 4, core: 2. Of those that a mesh axis runs over, the one named last changes fastest.
Arguments:
- queries: bfloat16 [3, 4096, 8192], P(None, 'seq', 'vocab'), may hold values from -32 to 32
- draft_kv: bfloat16 [3, 2, 4096, 1024], P(None, None, 'seq', 'vocab'), may hold values from -6 to 6
- doc_ids: int32 [4096], P('seq'), may hold values from 0 to 4, as said below
- logits: bfloat16 [4096, 65536], P('seq', 'vocab'), may hold values from -90 to 360
- targets: int32 [4096], P('seq'), may hold values from 0 to 65535
Outputs:
- attended: bfloat16 [3, 4096, 8192], P(None, 'seq', 'vocab')
- row_peak: float32 [3, 4096, 64], P(None, 'seq', 'vocab')
- token_loss: float32 [4096], P('seq')
Inputs may be any that keep to these rules, and one draw needn't show every extreme that they name: `doc_ids`: document ids start at 0, never fall, and rise by one where a new document begins; one document has exactly 3072 tokens, and the other tokens form exactly (4096 - 3072) // 256 documents, each shorter than it.
All inputs are finite; a program needn't handle non-finite values.
Results may differ from a plain program's by a relative error of at most 0.004.
Values may be sent and summed in bfloat16 or wider, within the bound.
No kernel may reach another device: no remote copies, remote signals or barrier semaphores. Data moves between devices by JAX's collectives and lax.ppermute only.
A program may use at most 128 MiB of HBM per device.

v0:
```python
import functools

import jax
import jax.numpy as jnp
from jax import lax
from jax.experimental import pallas as pl
from jax.experimental.pallas import tpu as pltpu
from jax.sharding import PartitionSpec as P


HD = 128
SUB = 16
LOG2E = 1.4426950408889634
FILL = -1e30
NT = (((1,), (1,)), ((), ()))
LIMIT = 100.0
KEEP = HD + 8
VMEM = 67043328
F32 = jnp.float32
BF16 = jnp.bfloat16


def pack_kernel(kvl, rows, kv_ref, doc_ref, out_ref, lst_ref):
    chunks = rows // HD
    along = jnp.broadcast_to(doc_ref[...].astype(F32), (rows, rows))
    lst_ref[...] = jnp.sum(jnp.where(along.T < along, 1.0, 0.0), axis=0, keepdims=True)
    for k in range(kvl):
        cols = slice(k * HD, (k + 1) * HD)
        out_ref[k, 0:rows, :] = kv_ref[0, 0, :, cols]
        vt = kv_ref[0, 1, :, cols].astype(F32).T.astype(BF16)
        docs = doc_ref[...].astype(F32).astype(BF16)
        for h in range(chunks):
            out_ref[k, rows + h * HD : rows + (h + 1) * HD, :] = vt[:, h * HD : (h + 1) * HD]
            out_ref[k, 2 * rows + h * SUB : 2 * rows + (h + 1) * SUB, :] = jnp.broadcast_to(
                docs[:, h * HD : (h + 1) * HD], (SUB, HD)
            )


def pack(draft_kv, doc_ids):
    rows = doc_ids.shape[0]
    kvl = draft_kv.shape[3] // HD
    depth = 2 * rows + SUB * (rows // HD)
    return pl.pallas_call(
        functools.partial(pack_kernel, kvl, rows),
        grid=(1,),
        out_shape=[
            jax.ShapeDtypeStruct((kvl, depth, HD), BF16),
            jax.ShapeDtypeStruct((1, rows), F32),
        ],
        in_specs=[
            pl.BlockSpec((1, 2, rows, kvl * HD), lambda i: (0, 0, 0, 0)),
            pl.BlockSpec((1, rows), lambda i: (0, 0)),
        ],
        out_specs=[
            pl.BlockSpec((kvl, depth, HD), lambda i: (0, 0, 0)),
            pl.BlockSpec((1, rows), lambda i: (0, 0)),
        ],
        name="pack",
    )(draft_kv, doc_ids.reshape(1, rows))


def stage_kernel(group, rows, steps, sources, first, chained, losses, doc_ref, *refs):
    refs = list(refs)
    last = losses > 0
    pairs = len(sources) // 2
    q_ref = refs.pop(0)
    blocks = [refs.pop(0) for _ in range(2 * pairs)]
    lst_ref = refs.pop(0)
    if first:
        own_ref = refs.pop(0)
    else:
        acc_in = refs.pop(0)
        top_in = refs.pop(0)
    if chained:
        refs = refs[2:]
    loss_refs = [refs.pop(0) for _ in range(losses)]
    if last:
        out_ref, peak_ref, loss_out, acc_out, top_out, q_all, count_ref, flag_ref = refs
    elif first:
        acc_out, top_out, own_s, q_all, count_ref, flag_ref = refs
    else:
        acc_out, top_out, q_all, count_ref, flag_ref = refs
    step = pl.program_id(1)
    opening = (pl.program_id(0) == 0) & (step == 0)
    scale = HD ** (-0.5)
    c2 = scale * LOG2E
    chunks = rows // HD
    lead = lst_ref[...] == 0.0
    for g in range(group):
        q_all[g] = q_ref[0, :, g * HD : (g + 1) * HD]

    @pl.when(opening)
    def _():
        me = lax.axis_index("seq")
        first_doc = doc_ref[0].astype(F32)
        for b, (flip, level) in enumerate(sources):
            source = (me ^ flip) - 4 * level
            below = jnp.zeros((SUB, HD), F32)
            for h in range(chunks):
                docs = blocks[b][0, 2 * rows + h * SUB : 2 * rows + (h + 1) * SUB, :].astype(F32)
                below = below + jnp.where(docs < first_doc, 1.0, 0.0)
            below = (jnp.sum(below) * (1.0 / SUB)).astype(jnp.int32)
            count_ref[b] = jnp.where((source >= 0) & (source < me), below, rows)

    if last:

        @pl.when(opening)
        def _():
            peak = functools.reduce(jnp.maximum, [r[0, 0:1, :] for r in loss_refs])
            total = sum(r[0, 1:2, :] * jnp.exp(r[0, 0:1, :] - peak) for r in loss_refs)
            loss_out[...] = peak + jnp.log(total) - sum(r[0, 2:3, :] for r in loss_refs)

    def values(b):
        parts = [blocks[b][0, rows + h * HD : rows + (h + 1) * HD, :] for h in range(chunks)]
        return jnp.concatenate([jnp.concatenate(parts, axis=1), jnp.ones((SUB, rows), BF16)], axis=0)

    def visit(pair, masked, fresh):
        pick = (2 * pair, 2 * pair + 1)
        vt = jnp.concatenate([values(b) for b in pick], axis=1)
        if masked:
            key_at = lax.broadcasted_iota(jnp.int32, (rows, rows), 0)
            ok = [key_at >= count_ref[b] for b in pick]
            if first:
                tok_at = lax.broadcasted_iota(jnp.int32, (rows, rows), 1)
                ok[0] = (key_at <= tok_at) & (key_at.astype(F32) >= lst_ref[...])
                ok[1] = ok[1] & lead
        waiting = []
        for g in range(group + 2):
            if g < group:
                ref = top_out[0, 0, g : g + 1, :]
                shift = (ref if first else jnp.where(lead, ref, -FILL)) * c2
                best = None
                probs = []
                for i, b in enumerate(pick):
                    s = lax.dot_general(
                        blocks[b][0, 0:rows, :], q_all[g], NT, preferred_element_type=F32
                    )
                    if masked:
                        s = jnp.where(ok[i], s, FILL)
                    m = jnp.max(s.reshape(rows // 8, 8, rows), axis=0)
                    best = m if best is None else jnp.maximum(best, m)
                    probs.append(jnp.exp2(s * c2 - shift).astype(BF16))
                best = jnp.max(best, axis=0, keepdims=True)
                if not first:
                    best = jnp.where(lead, best, FILL)
                top_out[0, 1, g : g + 1, :] = jnp.maximum(top_out[0, 1, g : g + 1, :], best)
                waiting.append((g, jnp.concatenate(probs, axis=0)))
            if g >= 2:
                w, p = waiting.pop(0)
                more = jnp.dot(vt, p, preferred_element_type=F32)[0:KEEP]
                if fresh:
                    acc_out[0, w] = acc_in[0, w] * top_out[0, 2, w : w + 1, :] + more
                else:
                    acc_out[0, w] = acc_out[0, w] + more

    def carry_over():
        for g in range(group):
            acc_out[0, g] = acc_in[0, g] * top_out[0, 2, g : g + 1, :]

    if first:

        ones = jnp.ones((SUB, HD), BF16)

        def diagonal(g, i):
            prod = q_all[g].astype(F32) * own_ref[i, 0].astype(F32)
            high = prod.astype(BF16)
            low = (prod - high.astype(F32)).astype(BF16)
            both = jnp.concatenate([high, low], axis=1)
            wide = jnp.concatenate([ones, ones], axis=1)
            return lax.dot_general(wide, both, NT, preferred_element_type=F32)[0:1]

        for i in range(1, steps):

            @pl.when(step >= i)
            def _():
                for g in range(group):
                    own_s[i, g : g + 1, :] = diagonal(g, i)

            @pl.when(step < i)
            def _():
                own_s[i] = jnp.full((group, rows), FILL, F32)

        for g in range(group):
            near = q_all[g] * own_ref[0, 0]
            own_s[0, g : g + 1, :] = lax.dot_general(ones, near, NT, preferred_element_type=F32)[0:1]
        top_out[0, 1] = functools.reduce(jnp.maximum, [own_s[i] for i in range(1, steps)])
        top_out[0, 0] = jnp.maximum(top_out[0, 1], own_s[0])

        def start():
            weights = [jnp.exp2((own_s[i] - top_out[0, 0]) * c2) for i in range(1, steps)]
            for g in range(group):
                acc_out[0, g, 0:HD] = jnp.zeros((HD, rows), F32)
                acc_out[0, g, HD:KEEP] = jnp.broadcast_to(
                    functools.reduce(jnp.add, weights)[g : g + 1, :], (KEEP - HD, rows)
                )
            for i in range(1, steps):

                @pl.when(step >= i)
                def _():
                    own_val = own_ref[i, 1].astype(F32).T
                    for g in range(group):
                        w = weights[i - 1][g : g + 1, :].astype(BF16).astype(F32)
                        acc_out[0, g, 0:HD] = acc_out[0, g, 0:HD] + own_val * w

    else:
        top_out[0, 0] = top_in[0, 0]
        top_out[0, 1] = top_in[0, 1]
        top_out[0, 2] = jnp.ones((group, rows), F32)

    flag_ref[0] = 1

    @pl.loop(0, 2)
    def _(_):
        @pl.when(flag_ref[0] == 1)
        def _():
            if first:
                start()
                visit(0, True, False)
            else:
                for pair in range(pairs):
                    a, b = count_ref[2 * pair], count_ref[2 * pair + 1]
                    some = jnp.minimum(a, b) < rows
                    full = jnp.maximum(a, b) == 0

                    @pl.when(full)
                    def _():
                        visit(pair, False, pair == 0)

                    @pl.when(some & jnp.logical_not(full))
                    def _():
                        visit(pair, True, pair == 0)

                    if pair == 0:

                        @pl.when(jnp.logical_not(some))
                        def _():
                            carry_over()

            over = jnp.max(top_out[0, 1] - top_out[0, 0]) * c2 > LIMIT
            flag_ref[0] = over.astype(jnp.int32)

            @pl.when(over)
            def _():
                top_out[0, 2] = jnp.exp2((top_out[0, 0] - top_out[0, 1]) * c2)
                top_out[0, 0] = top_out[0, 1]

    if last:
        for g in range(group):
            o = acc_out[0, g, 0:HD] * (1.0 / acc_out[0, g, HD : HD + 1])
            out_ref[0, :, g * HD : (g + 1) * HD] = o.T.astype(BF16)
        peak_ref[0] = top_out[0, 1] * scale


def stage(queries, draft_kv, doc_ids, blocks, lstart, sources, state, losses=(), heads=None):
    steps, rows, width = queries.shape
    kvl = draft_kv.shape[3] // HD
    group = width // HD // kvl
    depth = blocks[0].shape[1]
    first = heads is not None
    low, high = heads if first else (0, kvl)
    chained = first and state is not None
    last = len(losses) > 0
    acc_shape = (kvl * steps, group, KEEP, rows)
    top_shape = (kvl * steps, 3, group, rows)
    acc_spec = pl.BlockSpec((1, group, KEEP, rows), lambda k, j, s: ((k + low) * steps + j, 0, 0, 0))
    top_spec = pl.BlockSpec((1, 3, group, rows), lambda k, j, s: ((k + low) * steps + j, 0, 0, 0))
    row_spec = pl.BlockSpec((1, rows), lambda k, j, s: (0, 0))
    in_specs = (
        [pl.BlockSpec((1, rows, group * HD), lambda k, j, s: (j, 0, k + low))]
        + [pl.BlockSpec((1, depth, HD), lambda k, j, s: (k + low, 0, 0))] * len(blocks)
        + [row_spec]
    )
    args = [queries] + blocks + [lstart]
    scratch = [
        pltpu.VMEM((group, rows, HD), BF16),
        pltpu.SMEM((len(blocks),), jnp.int32),
        pltpu.SMEM((1,), jnp.int32),
    ]
    aliases = {}
    out_shape = [jax.ShapeDtypeStruct(acc_shape, F32), jax.ShapeDtypeStruct(top_shape, F32)]
    out_specs = [acc_spec, top_spec]
    if first:
        args += [draft_kv]
        in_specs += [pl.BlockSpec((steps, 2, rows, HD), lambda k, j, s: (0, 0, 0, k + low))]
        scratch = [pltpu.VMEM((steps, group, rows), F32)] + scratch
    if state is not None:
        aliases = {len(args) + 1: 0, len(args) + 2: 1}
        args += list(state)
        in_specs += [pl.BlockSpec(memory_space=pl.ANY)] * 2 if first else [acc_spec, top_spec]
    if last:
        aliases = {}
        args += losses
        in_specs += [pl.BlockSpec(losses[0].shape, lambda k, j, s: (0, 0, 0))] * len(losses)
        out_shape = [
            jax.ShapeDtypeStruct(queries.shape, BF16),
            jax.ShapeDtypeStruct((steps, kvl * group, rows), F32),
            jax.ShapeDtypeStruct((1, rows), F32),
        ]
        out_specs = [
            pl.BlockSpec((1, rows, group * HD), lambda k, j, s: (j, 0, k)),
            pl.BlockSpec((1, group, rows), lambda k, j, s: (j, k, 0)),
            row_spec,
        ]
        scratch = [
            pltpu.VMEM((1, group, KEEP, rows), F32),
            pltpu.VMEM((1, 3, group, rows), F32),
        ] + scratch
    work = (high - low) * steps * group * rows * rows * len(blocks)
    return pl.pallas_call(
        functools.partial(stage_kernel, group, rows, steps, sources, first, chained, len(losses)),
        out_shape=out_shape,
        grid_spec=pltpu.PrefetchScalarGridSpec(
            num_scalar_prefetch=1,
            grid=(high - low, steps),
            in_specs=in_specs,
            out_specs=out_specs,
            scratch_shapes=scratch,
        ),
        input_output_aliases=aliases,
        name="stage_first" if first else ("stage_last" if last else "stage_mid"),
        compiler_params=pltpu.CompilerParams(vmem_limit_bytes=VMEM),
        cost_estimate=pl.CostEstimate(
            flops=4 * work * HD, transcendentals=work, bytes_accessed=4 * kvl * steps * group * HD * rows
        ),
    )(doc_ids, *args)


def loss_kernel(block, width, tgt_ref, x_ref, out_ref, all_ref):
    i = pl.program_id(0)
    first = i * block
    start_col = lax.axis_index("vocab") * width
    step = min(width, 2048)
    wide = min(width, 512)
    row_at = lax.broadcasted_iota(jnp.int32, (SUB, HD), 0)
    lane_at = lax.broadcasted_iota(jnp.int32, (SUB, HD), 1)

    @pl.loop(0, block // SUB)
    def _(b):
        here = pl.ds(pl.multiple_of(b * SUB, SUB), SUB)
        peak = x_ref[here, 0:step]
        for c in range(1, width // step):
            peak = jnp.maximum(peak, x_ref[here, c * step : (c + 1) * step])
        peak = jnp.max(peak.astype(F32), axis=1, keepdims=True)
        total = jnp.zeros((SUB, wide), F32)
        for c in range(width // wide):
            x = x_ref[here, c * wide : (c + 1) * wide].astype(F32)
            total = total + jnp.exp2((x - peak) * LOG2E)
        total = jnp.sum(total, axis=1, keepdims=True)
        hit = jnp.zeros((SUB, HD), F32)
        for r in range(SUB):
            t = tgt_ref[first + b * SUB + r] - start_col
            inside = (t >= 0) & (t < width)
            lane = jnp.where(inside, t, 0)
            start = pl.multiple_of((lane // HD) * HD, HD)
            x = x_ref[here, pl.ds(start, HD)].astype(F32)
            hit = jnp.where((row_at == r) & (lane_at == lane - start) & inside, x, hit)
        hit = jnp.sum(hit, axis=1, keepdims=True)
        there = pl.ds(pl.multiple_of(first + b * SUB, SUB), SUB)
        all_ref[there, :] = jnp.where(lane_at == 0, peak, jnp.where(lane_at == 1, total, hit))

    @pl.when(i == pl.num_programs(0) - 1)
    def _():
        out_ref[0] = all_ref[...].T[0:8]


def loss_parts(logits, targets):
    rows, width = logits.shape
    block = 64
    return pl.pallas_call(
        functools.partial(loss_kernel, block, width),
        grid_spec=pltpu.PrefetchScalarGridSpec(
            num_scalar_prefetch=1,
            grid=(rows // block,),
            in_specs=[pl.BlockSpec((block, width), lambda i, t: (i, 0))],
            out_specs=pl.BlockSpec((1, 8, rows), lambda i, t: (0, 0, 0)),
            scratch_shapes=[pltpu.VMEM((rows, HD), F32)],
        ),
        out_shape=jax.ShapeDtypeStruct((1, 8, rows), F32),
        name="loss",
        compiler_params=pltpu.CompilerParams(vmem_limit_bytes=VMEM),
        cost_estimate=pl.CostEstimate(
            flops=4 * logits.size, transcendentals=logits.size, bytes_accessed=2 * logits.size
        ),
    )(targets, logits)


def program(queries, draft_kv, doc_ids, logits, targets):
    shards = lax.axis_size("seq")
    halves = lax.axis_size("vocab")
    levels = shards // 4

    def up(x):
        return lax.ppermute(x, "seq", [(i, i + 4) for i in range(shards - 4)])

    def swap(x, bit):
        return lax.ppermute(x, "seq", [(i, i ^ bit) for i in range(shards)])

    mine, lstart = pack(draft_kv, doc_ids)
    z, x, c, d = [mine], [], [], []

    def spread(level):
        if level + 1 < levels:
            z.append(up(z[level]))
        c.append(swap(z[level], 1))
        x.append(swap(z[level], 2))
        if level > 0:
            d.append(swap(x[level - 1], 1))
        if level + 1 == levels:
            d.append(swap(z[level], 3))

    spread(0)
    parts = loss_parts(logits, targets)
    z[1], x[0], parts = lax.optimization_barrier((z[1], x[0], parts))
    spread(1)
    losses = [parts] + [
        lax.ppermute(parts, "vocab", [(i, (i + t) % halves) for i in range(halves)])
        for t in range(1, halves)
    ]

    def run(picked, state, **more):
        names = {"z": (z, 0), "c": (c, 1), "x": (x, 2), "d": (d, 3)}
        blocks = [names[name][0][level] for name, level in picked]
        sources = [(names[name][1], level) for name, level in picked]
        return stage(queries, draft_kv, doc_ids, blocks, lstart, sources, state, **more)

    kvl = draft_kv.shape[3] // HD
    cuts = [0, kvl // 2, kvl] if kvl > 1 else [0, kvl]
    state = None
    for low, high in zip(cuts, cuts[1:]):
        state = run([("z", 0), ("c", 0)], state, heads=(low, high))
        level = len(c)
        if level < levels:
            z[level], x[level - 1], top = lax.optimization_barrier((z[level], x[level - 1], state[1]))
            state = [state[0], top]
            spread(level)
    while len(c) < levels:
        spread(len(c))
    rest = [("x", 0), ("d", 0)]
    for level in range(1, levels):
        rest += [(name, level) for name in "zcxd"]
    split = [0, 6] + list(range(14, len(rest) + 1, 8))
    for begin, end in zip(split, split[1:]):
        final = end == len(rest)
        state = run(rest[begin:end], state, losses=losses if final else [])
    out, peaks, token_loss = state
    return (out, peaks.transpose(0, 2, 1), token_loss.reshape(-1))


def solution(mesh):
    in_specs = (
        P(None, "seq", "vocab"),
        P(None, None, "seq", "vocab"),
        P("seq"),
        P("seq", "vocab"),
        P("seq"),
    )
    out_specs = (P(None, "seq", "vocab"), P(None, "seq", "vocab"), P("seq"))
    return jax.shard_map(program, mesh=mesh, in_specs=in_specs, out_specs=out_specs, check_vma=False)
```

profile of v0, /device:TPU:26, one launch (start us, length us, event | category | flops | bytes accessed | tf_op | source)
XLA Modules:
  0.0 176.5 jit_solution(9230330565610989687)
XLA Ops:
  0.6 2.0 %pack.1 = (bf16[4,544,128]{2,1,0:T(8,128)(2,1)}, f32[1,256]{1,0:T(1,128)}) custom-call(bf16[3,2,256,512]{3,2,1,0:T(8,128)(2,1)} %refs_4_.3, s32[1,256]{1,0:T(1,128)} %bitcast.3), custom_call_target="tpu_custom_call" | custom-call | tf_op jit(solution)/shard_map/pack/pallas_call | solution.py:43
  2.7 1.3 collective-permute-start
  4.0 0.6 collective-permute-start.1
  4.6 0.0 collective-permute-start.4
  4.6 12.2 %loss.1.refs_12_ = f32[1,8,256]{2,1,0:T(8,128)} custom-call(s32[256]{0:T(256)} %tgt_ref.1, bf16[256,32768]{1,0:T(8,128)(2,1)} %x_ref.1), custom_call_target="tpu_custom_call" | custom-call | flops 33554432 | bytes 16777216 | tf_op jit(solution)/shard_map/loss/pallas_call | solution.py:369
  16.8 2.4 %collective-permute-done.refs_3_ = bf16[4,544,128]{2,1,0:T(8,128)(2,1)} collective-permute-done((bf16[4,544,128]{2,1,0:T(8,128)(2,1)}, bf16[4,544,128]{2,1,0:T(8,128)(2,1)}, u32[]{:S(2)}, u32[]{:S(2)}) %collective-permute-start) | collective-permute-done | bytes 557088 | tf_op jit(solution)/shard_map/ppermute | solution.py:393
  19.2 0.0 collective-permute-done.1.refs_1_
  19.2 1.3 collective-permute-start.2
  20.5 0.6 collective-permute-start.3
  21.1 0.0 collective-permute-done.4.refs_2_
  21.1 17.1 %stage_first.2 = (f32[12,8,136,256]{3,2,1,0:T(8,128)}, f32[12,3,8,256]{3,2,1,0:T(8,128)}) custom-call(s32[256]{0:T(256)} %doc_ref.7, bf16[3,256,4096]{2,1,0:T(8,128)(2,1)} %refs_0_.7, bf16[4,544,128]{2,1,0:T(8,128)(2,1)} %get-tuple-element.23.refs_1_, bf16[4,544,128]{2,1,0:T(8,128)(2,1)} %collective-permute-done.4.refs_2_, ...), custom_call_target="tpu_custom_call" | custom-call | flops 3221225472 | bytes 12582912 | tf_op jit(solution)/shard_map/stage_first/pallas_call | solution.py:309
  38.3 0.0 collective-permute-done.2.refs_1_
  38.3 0.0 collective-permute-done.3.refs_5_
  38.3 1.5 collective-permute-start.6
  39.8 1.6 collective-permute-start.7
  41.3 0.0 collective-permute-start.13
  41.3 0.5 collective-permute-start.12
  41.8 0.0 collective-permute-start.14
  41.8 13.5 %collective-permute-done.6.refs_5_ = bf16[4,544,128]{2,1,0:T(8,128)(2,1)} collective-permute-done((bf16[4,544,128]{2,1,0:T(8,128)(2,1)}, bf16[4,544,128]{2,1,0:T(8,128)(2,1)}, u32[]{:S(2)}, u32[]{:S(2)}) %collective-permute-start.6) | collective-permute-done | bytes 557088 | tf_op jit(solution)/shard_map/ppermute | solution.py:393
  55.3 1.5 collective-permute-start.15
  56.8 17.2 %stage_first.3 = (f32[12,8,136,256]{3,2,1,0:T(8,128)}, f32[12,3,8,256]{3,2,1,0:T(8,128)}) custom-call(s32[256]{0:T(256)} %doc_ref.7, bf16[3,256,4096]{2,1,0:T(8,128)(2,1)} %refs_0_.7, bf16[4,544,128]{2,1,0:T(8,128)(2,1)} %get-tuple-element.23.refs_1_, ...), custom_call_target="tpu_custom_call", output_to_operand_aliasing={{0}: (6, {}), {1}: (7, {})} | custom-call | flops 3221225472 | bytes 12582912 | tf_op jit(solution)/shard_map/stage_first/pallas_call | solution.py:309
  74.0 0.0 collective-permute-done.7.refs_3_
  74.0 0.1 collective-permute-start.5
  74.1 0.0 collective-permute-done.15.refs_13_
  74.1 0.6 collective-permute-start.10
  74.7 0.0 collective-permute-done.13.refs_4_
  74.7 1.2 collective-permute-start.11
  76.0 0.0 collective-permute-done.12.refs_2_
  76.0 0.4 collective-permute-start.9
  76.4 0.0 collective-permute-done.14.refs_6_
  76.4 0.1 collective-permute-start.8
  76.5 47.3 %stage_mid.1 = (f32[12,8,136,256]{3,2,1,0:T(8,128)}, f32[12,3,8,256]{3,2,1,0:T(8,128)}) custom-call(s32[256]{0:T(256)} %doc_ref.7, bf16[3,256,4096]{2,1,0:T(8,128)(2,1)} %refs_0_.7, bf16[4,544,128]{2,1,0:T(8,128)(2,1)} %collective-permute-done.1.refs_1_, ...), custom_call_target="tpu_custom_call", output_to_operand_aliasing={{0}: (9, {}), {1}: (10, {})} | custom-call | flops 19327352832 | bytes 12582912 | tf_op jit(solution)/shard_map/stage_mid/pallas_call | solution.py:309
  123.8 0.0 collective-permute-done.5.refs_2_
  123.9 0.0 collective-permute-done.10.refs_7_
  123.9 0.0 collective-permute-done.11.refs_8_
  123.9 0.0 collective-permute-done.8.refs_4_
  123.9 0.0 collective-permute-done.9.refs_6_
  123.9 52.4 %stage_last.1 = (bf16[3,256,4096]{2,1,0:T(8,128)(2,1)}, f32[3,32,256]{2,1,0:T(8,128)}, f32[1,256]{1,0:T(1,128)}) custom-call(s32[256]{0:T(256)} %doc_ref.7, bf16[3,256,4096]{2,1,0:T(8,128)(2,1)} %refs_0_.7, bf16[4,544,128]{2,1,0:T(8,128)(2,1)} %collective-permute-done.2.refs_1_, bf16[4,544,128]{2,1,0:T(8,128)(2,1)} %collective-permute-done.5.refs_2_, ...), custom_call_target="tpu_custom_call" | custom-call | flops 25769803776 | bytes 12582912 | tf_op jit(solution)/shard_map/stage_last/pallas_call | solution.py:309
Async XLA Ops:
  2.7 16.6 %collective-permute-start = (bf16[4,544,128]{2,1,0:T(8,128)(2,1)}, bf16[4,544,128]{2,1,0:T(8,128)(2,1)}, u32[]{:S(2)}, u32[]{:S(2)}) collective-permute-start(bf16[4,544,128]{2,1,0:T(8,128)(2,1)} %get-tuple-element.23.refs_1_), channel_id=1, source_target_pairs={{0,8},{2,10},{4,12},{6,14},{8,16},{10,18},{12,20},{14,22},{16,24},... | collective-permute-start | bytes 1671176 | tf_op jit(solution)/shard_map/ppermute | solution.py:393
  4.0 15.3 %collective-permute-start.1 = (bf16[4,544,128]{2,1,0:T(8,128)(2,1)}, bf16[4,544,128]{2,1,0:T(8,128)(2,1)}, u32[]{:S(2)}, u32[]{:S(2)}) collective-permute-start(bf16[4,544,128]{2,1,0:T(8,128)(2,1)} %get-tuple-element.23.refs_1_), channel_id=1, source_target_pairs={{0,4},{2,6},{4,0},{6,2},{8,12},{10,14},{12,8},{14,10},{16,20},{18,... | collective-permute-start | bytes 1671176 | tf_op jit(solution)/shard_map/ppermute | solution.py:396
  4.6 16.6 %collective-permute-start.4 = (bf16[4,544,128]{2,1,0:T(8,128)(2,1)}, bf16[4,544,128]{2,1,0:T(8,128)(2,1)}, u32[]{:S(2)}, u32[]{:S(2)}) collective-permute-start(bf16[4,544,128]{2,1,0:T(8,128)(2,1)} %get-tuple-element.23.refs_1_), channel_id=1, source_target_pairs={{0,2},{2,0},{4,6},{6,4},{8,10},{10,8},{12,14},{14,12},{16,18},{18,... | collective-permute-start | bytes 1671176 | tf_op jit(solution)/shard_map/ppermute | solution.py:396
  19.2 19.0 %collective-permute-start.2 = (bf16[4,544,128]{2,1,0:T(8,128)(2,1)}, bf16[4,544,128]{2,1,0:T(8,128)(2,1)}, u32[]{:S(2)}, u32[]{:S(2)}) collective-permute-start(bf16[4,544,128]{2,1,0:T(8,128)(2,1)} %collective-permute-done.refs_3_), channel_id=1, source_target_pairs={{0,8},{2,10},{4,12},{6,14},{8,16},{10,18},{12,20},{14,22},{16,24},... | collective-permute-start | bytes 1671176 | tf_op jit(solution)/shard_map/ppermute | solution.py:393
  20.5 17.8 %collective-permute-start.3 = (bf16[4,544,128]{2,1,0:T(8,128)(2,1)}, bf16[4,544,128]{2,1,0:T(8,128)(2,1)}, u32[]{:S(2)}, u32[]{:S(2)}) collective-permute-start(bf16[4,544,128]{2,1,0:T(8,128)(2,1)} %collective-permute-done.refs_3_), channel_id=1, source_target_pairs={{0,4},{2,6},{4,0},{6,2},{8,12},{10,14},{12,8},{14,10},{16,20},{18,... | collective-permute-start | bytes 1671176 | tf_op jit(solution)/shard_map/ppermute | solution.py:396
  38.3 17.0 %collective-permute-start.6 = (bf16[4,544,128]{2,1,0:T(8,128)(2,1)}, bf16[4,544,128]{2,1,0:T(8,128)(2,1)}, u32[]{:S(2)}, u32[]{:S(2)}) collective-permute-start(bf16[4,544,128]{2,1,0:T(8,128)(2,1)} %collective-permute-done.2.refs_1_), channel_id=1, source_target_pairs={{0,8},{2,10},{4,12},{6,14},{8,16},{10,18},{12,20},{14,22},{16,24},... | collective-permute-start | bytes 1671176 | tf_op jit(solution)/shard_map/ppermute | solution.py:393
  39.8 34.3 %collective-permute-start.7 = (bf16[4,544,128]{2,1,0:T(8,128)(2,1)}, bf16[4,544,128]{2,1,0:T(8,128)(2,1)}, u32[]{:S(2)}, u32[]{:S(2)}) collective-permute-start(bf16[4,544,128]{2,1,0:T(8,128)(2,1)} %collective-permute-done.2.refs_1_), channel_id=1, source_target_pairs={{0,4},{2,6},{4,0},{6,2},{8,12},{10,14},{12,8},{14,10},{16,20},{18,... | collective-permute-start | bytes 1671176 | tf_op jit(solution)/shard_map/ppermute | solution.py:396
  41.3 33.4 %collective-permute-start.13 = (bf16[4,544,128]{2,1,0:T(8,128)(2,1)}, bf16[4,544,128]{2,1,0:T(8,128)(2,1)}, u32[]{:S(2)}, u32[]{:S(2)}) collective-permute-start(bf16[4,544,128]{2,1,0:T(8,128)(2,1)} %collective-permute-done.refs_3_), channel_id=1, source_target_pairs={{0,2},{2,0},{4,6},{6,4},{8,10},{10,8},{12,14},{14,12},{16,18},{18,... | collective-permute-start | bytes 1671176 | tf_op jit(solution)/shard_map/ppermute | solution.py:396
  41.3 34.7 %collective-permute-start.12 = (bf16[4,544,128]{2,1,0:T(8,128)(2,1)}, bf16[4,544,128]{2,1,0:T(8,128)(2,1)}, u32[]{:S(2)}, u32[]{:S(2)}) collective-permute-start(bf16[4,544,128]{2,1,0:T(8,128)(2,1)} %collective-permute-done.1.refs_1_), channel_id=1, source_target_pairs={{0,2},{2,0},{4,6},{6,4},{8,10},{10,8},{12,14},{14,12},{16,18},{18,... | collective-permute-start | bytes 1671176 | tf_op jit(solution)/shard_map/ppermute | solution.py:396
  41.8 34.5 %collective-permute-start.14 = (bf16[4,544,128]{2,1,0:T(8,128)(2,1)}, bf16[4,544,128]{2,1,0:T(8,128)(2,1)}, u32[]{:S(2)}, u32[]{:S(2)}) collective-permute-start(bf16[4,544,128]{2,1,0:T(8,128)(2,1)} %collective-permute-done.3.refs_5_), channel_id=1, source_target_pairs={{0,2},{2,0},{4,6},{6,4},{8,10},{10,8},{12,14},{14,12},{16,18},{18,... | collective-permute-start | bytes 1671176 | tf_op jit(solution)/shard_map/ppermute | solution.py:396
  55.3 18.8 %collective-permute-start.15 = (f32[1,8,256]{2,1,0:T(8,128)}, f32[1,8,256]{2,1,0:T(8,128)}, u32[]{:S(2)}, u32[]{:S(2)}) collective-permute-start(f32[1,8,256]{2,1,0:T(8,128)} %loss.1.refs_12_), channel_id=1, source_target_pairs={{0,1},{1,0},{2,3},{3,2},{4,5},{5,4},{6,7},{7,6},{8,9},{9,8},{10,11... | collective-permute-start | bytes 24584 | tf_op jit(solution)/shard_map/ppermute | solution.py:416
  74.0 49.8 %collective-permute-start.5 = (bf16[4,544,128]{2,1,0:T(8,128)(2,1)}, bf16[4,544,128]{2,1,0:T(8,128)(2,1)}, u32[]{:S(2)}, u32[]{:S(2)}) collective-permute-start(bf16[4,544,128]{2,1,0:T(8,128)(2,1)} %collective-permute-done.2.refs_1_), channel_id=1, source_target_pairs={{0,2},{2,0},{4,6},{6,4},{8,10},{10,8},{12,14},{14,12},{16,18},{18,... | collective-permute-start | bytes 1671176 | tf_op jit(solution)/shard_map/ppermute | solution.py:396
  74.1 49.7 %collective-permute-start.10 = (bf16[4,544,128]{2,1,0:T(8,128)(2,1)}, bf16[4,544,128]{2,1,0:T(8,128)(2,1)}, u32[]{:S(2)}, u32[]{:S(2)}) collective-permute-start(bf16[4,544,128]{2,1,0:T(8,128)(2,1)} %collective-permute-done.6.refs_5_), channel_id=1, source_target_pairs={{0,4},{2,6},{4,0},{6,2},{8,12},{10,14},{12,8},{14,10},{16,20},{18,... | collective-permute-start | bytes 1671176 | tf_op jit(solution)/shard_map/ppermute | solution.py:396
  74.7 49.1 %collective-permute-start.11 = (bf16[4,544,128]{2,1,0:T(8,128)(2,1)}, bf16[4,544,128]{2,1,0:T(8,128)(2,1)}, u32[]{:S(2)}, u32[]{:S(2)}) collective-permute-start(bf16[4,544,128]{2,1,0:T(8,128)(2,1)} %collective-permute-done.6.refs_5_), channel_id=1, source_target_pairs={{0,6},{2,4},{4,2},{6,0},{8,14},{10,12},{12,10},{14,8},{16,22},{18,... | collective-permute-start | bytes 1671176 | tf_op jit(solution)/shard_map/ppermute | solution.py:396
  76.0 47.9 %collective-permute-start.9 = (bf16[4,544,128]{2,1,0:T(8,128)(2,1)}, bf16[4,544,128]{2,1,0:T(8,128)(2,1)}, u32[]{:S(2)}, u32[]{:S(2)}) collective-permute-start(bf16[4,544,128]{2,1,0:T(8,128)(2,1)} %collective-permute-done.6.refs_5_), channel_id=1, source_target_pairs={{0,2},{2,0},{4,6},{6,4},{8,10},{10,8},{12,14},{14,12},{16,18},{18,... | collective-permute-start | bytes 1671176 | tf_op jit(solution)/shard_map/ppermute | solution.py:396
  76.4 47.5 %collective-permute-start.8 = (bf16[4,544,128]{2,1,0:T(8,128)(2,1)}, bf16[4,544,128]{2,1,0:T(8,128)(2,1)}, u32[]{:S(2)}, u32[]{:S(2)}) collective-permute-start(bf16[4,544,128]{2,1,0:T(8,128)(2,1)} %collective-permute-done.7.refs_3_), channel_id=1, source_target_pairs={{0,2},{2,0},{4,6},{6,4},{8,10},{10,8},{12,14},{14,12},{16,18},{18,... | collective-permute-start | bytes 1671176 | tf_op jit(solution)/shard_map/ppermute | solution.py:396
where the time goes:
time: 177 us; the launch traced here: 176 us
  Pallas kernels  148 us (84%)
  waiting for transfers between devices  15.9 us (9%)
  starting transfers between devices  11.3 us (6%)
    pallas_call x4, Pallas kernels, stage(): pl.pallas_call(functools.partial(stage_kernel, group, rows, steps, source...  134 us
    ppermute x3, waiting for transfers between devices, up(): return lax.ppermute(x, 'seq', [(i, i + 4) for i in range(shards - 4)])  15.9 us
    pallas_call x1, Pallas kernels, loss_parts(): pl.pallas_call(functools.partial(loss_kernel, block, width), grid_spec=pl...  12.2 us
    ppermute x12, starting transfers between devices, swap(): return lax.ppermute(x, 'seq', [(i, i ^ bit) for i in range(shards)])  5.7 us
    ppermute x3, starting transfers between devices, up(): return lax.ppermute(x, 'seq', [(i, i + 4) for i in range(shards - 4)])  4.03 us
  transfers between devices with their start and end apart: 16, of which 2 were waited for; matrix products, arithmetic and copies ran while one was open for 0% of the time, Pallas kernels for 53%

commit v1 on v0

--- a/solution.py
+++ b/solution.py
@@ -13,7 +13,7 @@
 LOG2E = 1.4426950408889634
 FILL = -1e30
 NT = (((1,), (1,)), ((), ()))
-LIMIT = 100.0
+LIMIT = 60.0
 KEEP = HD + 8
 VMEM = 67043328
 F32 = jnp.float32
@@ -75,11 +75,11 @@
         refs = refs[2:]
     loss_refs = [refs.pop(0) for _ in range(losses)]
     if last:
-        out_ref, peak_ref, loss_out, acc_out, top_out, q_all, count_ref, flag_ref = refs
+        out_ref, peak_ref, loss_out, acc_out, top_out, q_all, count_ref = refs
     elif first:
-        acc_out, top_out, own_s, q_all, count_ref, flag_ref = refs
+        acc_out, top_out, own_s, bias_ref, q_all, count_ref = refs
     else:
-        acc_out, top_out, q_all, count_ref, flag_ref = refs
+        acc_out, top_out, q_all, count_ref = refs
     step = pl.program_id(1)
     opening = (pl.program_id(0) == 0) & (step == 0)
     scale = HD ** (-0.5)
@@ -112,52 +112,91 @@
 
     def values(b):
         parts = [blocks[b][0, rows + h * HD : rows + (h + 1) * HD, :] for h in range(chunks)]
-        return jnp.concatenate([jnp.concatenate(parts, axis=1), jnp.ones((SUB, rows), BF16)], axis=0)
-
-    def visit(pair, masked, fresh):
-        pick = (2 * pair, 2 * pair + 1)
-        vt = jnp.concatenate([values(b) for b in pick], axis=1)
-        if masked:
-            key_at = lax.broadcasted_iota(jnp.int32, (rows, rows), 0)
-            ok = [key_at >= count_ref[b] for b in pick]
-            if first:
-                tok_at = lax.broadcasted_iota(jnp.int32, (rows, rows), 1)
-                ok[0] = (key_at <= tok_at) & (key_at.astype(F32) >= lst_ref[...])
-                ok[1] = ok[1] & lead
+        return jnp.concatenate(parts, axis=1)
+
+    def folded(v, op):
+        return op(v.reshape(rows // 8, 8, rows), axis=0)
+
+    def usable(pair):
+        key_at = lax.broadcasted_iota(jnp.int32, (rows, rows), 0)
+        ok = [key_at >= count_ref[2 * pair + i] for i in range(2)]
+        if first:
+            tok_at = lax.broadcasted_iota(jnp.int32, (rows, rows), 1)
+            ok[0] = (key_at <= tok_at) & (key_at.astype(F32) >= lst_ref[...])
+            ok[1] = ok[1] & lead
+        return ok
+
+    def scores(pair, i, q):
+        return lax.dot_general(
+            blocks[2 * pair + i][0, 0:rows, :], q, NT, preferred_element_type=F32
+        )
+
+    def pair_values(pair):
+        return jnp.concatenate([values(2 * pair), values(2 * pair + 1)], axis=1)
+
+    def visit(chosen, masked, fresh):
+        units = [(g, pair) for g in range(group) for pair in chosen]
+        vts = {pair: pair_values(pair) for pair in chosen}
+        oks = {pair: usable(pair) for pair in chosen} if masked and not first else {}
+        best, sums = {}, {}
         waiting = []
-        for g in range(group + 2):
-            if g < group:
-                ref = top_out[0, 0, g : g + 1, :]
-                shift = (ref if first else jnp.where(lead, ref, -FILL)) * c2
-                best = None
+        for n in range(len(units) + 2):
+            if n < len(units):
+                g, pair = units[n]
                 probs = []
-                for i, b in enumerate(pick):
-                    s = lax.dot_general(
-                        blocks[b][0, 0:rows, :], q_all[g], NT, preferred_element_type=F32
+                for i in range(2):
+                    s = scores(pair, i, q_all[g])
+                    if first:
+                        s = s + bias_ref[i]
+                    elif masked:
+                        s = jnp.where(oks[pair][i], s, FILL)
+                    m = folded(s, jnp.max)
+                    best[g] = jnp.maximum(best[g], m) if g in best else m
+                    p = jnp.exp2(s * c2)
+                    t = folded(p, jnp.sum)
+                    sums[g] = sums[g] + t if g in sums else t
+                    probs.append(p.astype(BF16))
+                if pair == chosen[-1]:
+                    peak = jnp.max(best.pop(g), axis=0, keepdims=True)
+                    if not first:
+                        peak = jnp.where(lead, peak, FILL)
+                    top_out[0, 1, g : g + 1, :] = jnp.maximum(top_out[0, 1, g : g + 1, :], peak)
+                waiting.append((g, pair, jnp.concatenate(probs, axis=0)))
+            if n >= 2:
+                g, pair, p = waiting.pop(0)
+                more = jnp.dot(vts[pair], p, preferred_element_type=F32)
+                old = acc_in if fresh and pair == chosen[0] else acc_out
+                acc_out[0, g, 0:HD] = old[0, g, 0:HD] + (more if first else jnp.where(lead, more, 0.0))
+                if pair == chosen[-1]:
+                    more = sums.pop(g)
+                    old = acc_in if fresh else acc_out
+                    acc_out[0, g, HD:KEEP] = old[0, g, HD:KEEP] + (
+                        more if first else jnp.where(lead, more, 0.0)
                     )
-                    if masked:
-                        s = jnp.where(ok[i], s, FILL)
-                    m = jnp.max(s.reshape(rows // 8, 8, rows), axis=0)
-                    best = m if best is None else jnp.maximum(best, m)
-                    probs.append(jnp.exp2(s * c2 - shift).astype(BF16))
-                best = jnp.max(best, axis=0, keepdims=True)
-                if not first:
-                    best = jnp.where(lead, best, FILL)
-                top_out[0, 1, g : g + 1, :] = jnp.maximum(top_out[0, 1, g : g + 1, :], best)
-                waiting.append((g, jnp.concatenate(probs, axis=0)))
-            if g >= 2:
-                w, p = waiting.pop(0)
-                more = jnp.dot(vt, p, preferred_element_type=F32)[0:KEEP]
-                if fresh:
-                    acc_out[0, w] = acc_in[0, w] * top_out[0, 2, w : w + 1, :] + more
-                else:
-                    acc_out[0, w] = acc_out[0, w] + more
-
-    def carry_over():
-        for g in range(group):
-            acc_out[0, g] = acc_in[0, g] * top_out[0, 2, g : g + 1, :]
+
+    def revisit(pair):
+        ok = usable(pair)
+        if not first:
+            ok = [one & lead for one in ok]
+        vt = pair_values(pair)
+
+        @pl.loop(0, group)
+        def _(g):
+            shift = top_out[0, 0, pl.ds(g, 1), :] * c2
+            probs = [
+                jnp.exp2(jnp.where(ok[i], scores(pair, i, q_all[g]), FILL) * c2 - shift) for i in range(2)
+            ]
+            acc_out[0, g, HD:KEEP] = acc_out[0, g, HD:KEEP] + sum(folded(p, jnp.sum) for p in probs)
+            p = jnp.concatenate(probs, axis=0).astype(BF16)
+            acc_out[0, g, 0:HD] = acc_out[0, g, 0:HD] + jnp.dot(vt, p, preferred_element_type=F32)
 
     if first:
+
+        @pl.when(opening)
+        def _():
+            for i, ok in enumerate(usable(0)):
+                bias_ref[i] = jnp.where(ok, 0.0, FILL)
+
 
         ones = jnp.ones((SUB, HD), BF16)
 
@@ -180,18 +219,15 @@
             def _():
                 own_s[i] = jnp.full((group, rows), FILL, F32)
 
-        for g in range(group):
-            near = q_all[g] * own_ref[0, 0]
-            own_s[0, g : g + 1, :] = lax.dot_general(ones, near, NT, preferred_element_type=F32)[0:1]
+        top_out[0, 0] = jnp.zeros((group, rows), F32)
         top_out[0, 1] = functools.reduce(jnp.maximum, [own_s[i] for i in range(1, steps)])
-        top_out[0, 0] = jnp.maximum(top_out[0, 1], own_s[0])
 
         def start():
             weights = [jnp.exp2((own_s[i] - top_out[0, 0]) * c2) for i in range(1, steps)]
             for g in range(group):
                 acc_out[0, g, 0:HD] = jnp.zeros((HD, rows), F32)
                 acc_out[0, g, HD:KEEP] = jnp.broadcast_to(
-                    functools.reduce(jnp.add, weights)[g : g + 1, :], (KEEP - HD, rows)
+                    functools.reduce(jnp.add, weights)[g : g + 1, :] * (1.0 / (KEEP - HD)), (KEEP - HD, rows)
                 )
             for i in range(1, steps):
 
@@ -202,51 +238,59 @@
                         w = weights[i - 1][g : g + 1, :].astype(BF16).astype(F32)
                         acc_out[0, g, 0:HD] = acc_out[0, g, 0:HD] + own_val * w
 
+        start()
+        visit([0], True, False)
+        spread = jnp.max(jnp.abs(top_out[0, 1])) * c2
+
+        @pl.when(spread > LIMIT)
+        def _():
+            top_out[0, 0] = top_out[0, 1]
+            start()
+            revisit(0)
+
     else:
-        top_out[0, 0] = top_in[0, 0]
-        top_out[0, 1] = top_in[0, 1]
-        top_out[0, 2] = jnp.ones((group, rows), F32)
-
-    flag_ref[0] = 1
-
-    @pl.loop(0, 2)
-    def _(_):
-        @pl.when(flag_ref[0] == 1)
+        top_out[...] = top_in[...]
+        some, full = [], []
+        for pair in range(pairs):
+            a, b = count_ref[2 * pair], count_ref[2 * pair + 1]
+            some.append(jnp.minimum(a, b) < rows)
+            full.append(jnp.maximum(a, b) == 0)
+        joined = list(range(2 if last else pairs))
+        all_full = functools.reduce(jnp.logical_and, [full[pair] for pair in joined])
+
+        @pl.when(all_full)
         def _():
-            if first:
-                start()
-                visit(0, True, False)
-            else:
-                for pair in range(pairs):
-                    a, b = count_ref[2 * pair], count_ref[2 * pair + 1]
-                    some = jnp.minimum(a, b) < rows
-                    full = jnp.maximum(a, b) == 0
-
-                    @pl.when(full)
-                    def _():
-                        visit(pair, False, pair == 0)
-
-                    @pl.when(some & jnp.logical_not(full))
-                    def _():
-                        visit(pair, True, pair == 0)
-
-                    if pair == 0:
-
-                        @pl.when(jnp.logical_not(some))
-                        def _():
-                            carry_over()
-
-            over = jnp.max(top_out[0, 1] - top_out[0, 0]) * c2 > LIMIT
-            flag_ref[0] = over.astype(jnp.int32)
-
-            @pl.when(over)
+            visit(joined, False, True)
+
+        @pl.when(jnp.logical_not(all_full))
+        def _():
+            for g in range(group):
+                acc_out[0, g] = acc_in[0, g]
+
+        for pair in range(pairs):
+
+            @pl.when(some[pair] & jnp.logical_not(all_full & (pair in joined)))
             def _():
-                top_out[0, 2] = jnp.exp2((top_out[0, 0] - top_out[0, 1]) * c2)
-                top_out[0, 0] = top_out[0, 1]
+                visit([pair], True, False)
+
+        past = top_in[0, 0]
+        spread = jnp.maximum(jnp.max(top_out[0, 1]) * c2 - LIMIT, jnp.max(jnp.abs(past)))
+
+        @pl.when(spread > 0.0)
+        def _():
+            top_out[0, 0] = top_out[0, 1]
+            fade = jnp.exp2((past - top_out[0, 1]) * c2)
+            for g in range(group):
+                acc_out[0, g] = acc_in[0, g] * fade[g : g + 1, :]
+            for pair in range(pairs):
+
+                @pl.when(some[pair])
+                def _():
+                    revisit(pair)
 
     if last:
         for g in range(group):
-            o = acc_out[0, g, 0:HD] * (1.0 / acc_out[0, g, HD : HD + 1])
+            o = acc_out[0, g, 0:HD] * (1.0 / jnp.sum(acc_out[0, g, HD:KEEP], axis=0, keepdims=True))
             out_ref[0, :, g * HD : (g + 1) * HD] = o.T.astype(BF16)
         peak_ref[0] = top_out[0, 1] * scale
 
@@ -261,9 +305,9 @@
     chained = first and state is not None
     last = len(losses) > 0
     acc_shape = (kvl * steps, group, KEEP, rows)
-    top_shape = (kvl * steps, 3, group, rows)
+    top_shape = (kvl * steps, 2, group, rows)
     acc_spec = pl.BlockSpec((1, group, KEEP, rows), lambda k, j, s: ((k + low) * steps + j, 0, 0, 0))
-    top_spec = pl.BlockSpec((1, 3, group, rows), lambda k, j, s: ((k + low) * steps + j, 0, 0, 0))
+    top_spec = pl.BlockSpec((1, 2, group, rows), lambda k, j, s: ((k + low) * steps + j, 0, 0, 0))
     row_spec = pl.BlockSpec((1, rows), lambda k, j, s: (0, 0))
     in_specs = (
         [pl.BlockSpec((1, rows, group * HD), lambda k, j, s: (j, 0, k + low))]
@@ -274,7 +318,6 @@
     scratch = [
         pltpu.VMEM((group, rows, HD), BF16),
         pltpu.SMEM((len(blocks),), jnp.int32),
-        pltpu.SMEM((1,), jnp.int32),
     ]
     aliases = {}
     out_shape = [jax.ShapeDtypeStruct(acc_shape, F32), jax.ShapeDtypeStruct(top_shape, F32)]
@@ -282,7 +325,10 @@
     if first:
         args += [draft_kv]
         in_specs += [pl.BlockSpec((steps, 2, rows, HD), lambda k, j, s: (0, 0, 0, k + low))]
-        scratch = [pltpu.VMEM((steps, group, rows), F32)] + scratch
+        scratch = [
+            pltpu.VMEM((steps, group, rows), F32),
+            pltpu.VMEM((2, rows, rows), F32),
+        ] + scratch
     if state is not None:
         aliases = {len(args) + 1: 0, len(args) + 2: 1}
         args += list(state)
@@ -303,7 +349,7 @@
         ]
         scratch = [
             pltpu.VMEM((1, group, KEEP, rows), F32),
-            pltpu.VMEM((1, 3, group, rows), F32),
+            pltpu.VMEM((1, 2, group, rows), F32),
         ] + scratch
     work = (high - low) * steps * group * rows * rows * len(blocks)
     return pl.pallas_call(

time: 177 us -> 467 us (2.64)
  Pallas kernels: 148 us -> 438 us
    pallas_call x4, Pallas kernels: 134 us -> 424 us  [stage(): pl.pallas_call(functools.partial(stage_kernel, group, rows, steps, source...]
  transfers between devices with their start and end apart: 16 -> 16, of which waited for: 2 -> 2; matrix products, arithmetic and copies ran while one was open for 0% -> 0% of each run, Pallas kernels for 53% -> 55%
where the time goes in v1:
time: 467 us; the launch traced here: 466 us
  Pallas kernels  438 us (94%)
  waiting for transfers between devices  16 us (3%)
  starting transfers between devices  11.3 us (2%)
    pallas_call x4, Pallas kernels, stage(): pl.pallas_call(functools.partial(stage_kernel, group, rows, steps, source...  424 us
    ppermute x3, waiting for transfers between devices, up(): return lax.ppermute(x, 'seq', [(i, i + 4) for i in range(shards - 4)])  15.9 us
    pallas_call x1, Pallas kernels, loss_parts(): pl.pallas_call(functools.partial(loss_kernel, block, width), grid_spec=pl...  12.2 us
  transfers between devices with their start and end apart: 16, of which 2 were waited for; matrix products, arithmetic and copies ran while one was open for 0% of the time, Pallas kernels for 55%

profile of v1, /device:TPU:26, one launch (start us, length us, event | category | flops | bytes accessed | tf_op | source)
XLA Modules:
  0.0 466.3 jit_solution(18189985568635872494)
XLA Ops:
  0.6 2.0 pack.1
  2.7 1.3 collective-permute-start
  4.0 0.6 collective-permute-start.1
  4.6 0.0 collective-permute-start.4
  4.6 12.2 %loss.1.refs_12_ = f32[1,8,256]{2,1,0:T(8,128)} custom-call(s32[256]{0:T(256)} %tgt_ref.1, bf16[256,32768]{1,0:T(8,128)(2,1)} %x_ref.1), custom_call_target="tpu_custom_call" | custom-call | flops 33554432 | bytes 16777216 | tf_op jit(solution)/shard_map/loss/pallas_call | solution.py:415
  16.8 2.4 collective-permute-done.refs_3_
  19.2 0.0 collective-permute-done.1.refs_1_
  19.2 1.3 collective-permute-start.2
  20.5 0.6 collective-permute-start.3
  21.1 0.0 collective-permute-done.4.refs_2_
  21.1 37.2 %stage_first.2 = (f32[12,8,136,256]{3,2,1,0:T(8,128)}, f32[12,2,8,256]{3,2,1,0:T(8,128)}) custom-call(s32[256]{0:T(256)} %doc_ref.7, bf16[3,256,4096]{2,1,0:T(8,128)(2,1)} %refs_0_.7, bf16[4,544,128]{2,1,0:T(8,128)(2,1)} %get-tuple-element.23.refs_1_, bf16[4,544,128]{2,1,0:T(8,128)(2,1)} %collective-permute-done.4.refs_2_, ...), custom_call_target="tpu_custom_call" | custom-call | flops 3221225472 | bytes 12582912 | tf_op jit(solution)/shard_map/stage_first/pallas_call | solution.py:355
  58.3 0.0 collective-permute-done.2.refs_1_
  58.3 0.0 collective-permute-done.3.refs_5_
  58.3 1.5 collective-permute-start.6
  59.8 1.6 collective-permute-start.7
  61.3 0.0 collective-permute-start.13
  61.4 0.5 collective-permute-start.12
  61.9 0.0 collective-permute-start.14
  61.9 13.5 %collective-permute-done.6.refs_5_ = bf16[4,544,128]{2,1,0:T(8,128)(2,1)} collective-permute-done((bf16[4,544,128]{2,1,0:T(8,128)(2,1)}, bf16[4,544,128]{2,1,0:T(8,128)(2,1)}, u32[]{:S(2)}, u32[]{:S(2)}) %collective-permute-start.6) | collective-permute-done | bytes 557088 | tf_op jit(solution)/shard_map/ppermute | solution.py:439
  75.4 1.5 collective-permute-start.15
  76.9 37.2 %stage_first.3 = (f32[12,8,136,256]{3,2,1,0:T(8,128)}, f32[12,2,8,256]{3,2,1,0:T(8,128)}) custom-call(s32[256]{0:T(256)} %doc_ref.7, bf16[3,256,4096]{2,1,0:T(8,128)(2,1)} %refs_0_.7, bf16[4,544,128]{2,1,0:T(8,128)(2,1)} %get-tuple-element.23.refs_1_, ...), custom_call_target="tpu_custom_call", output_to_operand_aliasing={{0}: (6, {}), {1}: (7, {})} | custom-call | flops 3221225472 | bytes 12582912 | tf_op jit(solution)/shard_map/stage_first/pallas_call | solution.py:355
  114.1 0.0 collective-permute-done.7.refs_3_
  114.1 0.1 collective-permute-start.5
  114.1 0.0 collective-permute-done.15.refs_13_
  114.1 0.6 collective-permute-start.10
  114.7 0.0 collective-permute-done.13.refs_4_
  114.7 1.2 collective-permute-start.11
  116.0 0.0 collective-permute-done.12.refs_2_
  116.0 0.4 collective-permute-start.9
  116.4 0.0 collective-permute-done.14.refs_6_
  116.4 0.1 collective-permute-start.8
  116.5 170.8 %stage_mid.1 = (f32[12,8,136,256]{3,2,1,0:T(8,128)}, f32[12,2,8,256]{3,2,1,0:T(8,128)}) custom-call(s32[256]{0:T(256)} %doc_ref.7, bf16[3,256,4096]{2,1,0:T(8,128)(2,1)} %refs_0_.7, bf16[4,544,128]{2,1,0:T(8,128)(2,1)} %collective-permute-done.1.refs_1_, ...), custom_call_target="tpu_custom_call", output_to_operand_aliasing={{0}: (9, {}), {1}: (10, {})} | custom-call | flops 19327352832 | bytes 12582912 | tf_op jit(solution)/shard_map/stage_mid/pallas_call | solution.py:355
  287.3 0.0 collective-permute-done.5.refs_2_
  287.3 0.0 collective-permute-done.10.refs_7_
  287.3 0.0 collective-permute-done.11.refs_8_
  287.3 0.0 collective-permute-done.8.refs_4_
  287.3 0.0 collective-permute-done.9.refs_6_
  287.3 178.8 %stage_last.1 = (bf16[3,256,4096]{2,1,0:T(8,128)(2,1)}, f32[3,32,256]{2,1,0:T(8,128)}, f32[1,256]{1,0:T(1,128)}) custom-call(s32[256]{0:T(256)} %doc_ref.7, bf16[3,256,4096]{2,1,0:T(8,128)(2,1)} %refs_0_.7, bf16[4,544,128]{2,1,0:T(8,128)(2,1)} %collective-permute-done.2.refs_1_, bf16[4,544,128]{2,1,0:T(8,128)(2,1)} %collective-permute-done.5.refs_2_, ...), custom_call_target="tpu_custom_call" | custom-call | flops 25769803776 | bytes 12582912 | tf_op jit(solution)/shard_map/stage_last/pallas_call | solution.py:355
Async XLA Ops:
  2.7 16.6 %collective-permute-start = (bf16[4,544,128]{2,1,0:T(8,128)(2,1)}, bf16[4,544,128]{2,1,0:T(8,128)(2,1)}, u32[]{:S(2)}, u32[]{:S(2)}) collective-permute-start(bf16[4,544,128]{2,1,0:T(8,128)(2,1)} %get-tuple-element.23.refs_1_), channel_id=1, source_target_pairs={{0,8},{2,10},{4,12},{6,14},{8,16},{10,18},{12,20},{14,22},{16,24},... | collective-permute-start | bytes 1671176 | tf_op jit(solution)/shard_map/ppermute | solution.py:439
  4.0 15.3 %collective-permute-start.1 = (bf16[4,544,128]{2,1,0:T(8,128)(2,1)}, bf16[4,544,128]{2,1,0:T(8,128)(2,1)}, u32[]{:S(2)}, u32[]{:S(2)}) collective-permute-start(bf16[4,544,128]{2,1,0:T(8,128)(2,1)} %get-tuple-element.23.refs_1_), channel_id=1, source_target_pairs={{0,4},{2,6},{4,0},{6,2},{8,12},{10,14},{12,8},{14,10},{16,20},{18,... | collective-permute-start | bytes 1671176 | tf_op jit(solution)/shard_map/ppermute | solution.py:442
  4.6 16.6 %collective-permute-start.4 = (bf16[4,544,128]{2,1,0:T(8,128)(2,1)}, bf16[4,544,128]{2,1,0:T(8,128)(2,1)}, u32[]{:S(2)}, u32[]{:S(2)}) collective-permute-start(bf16[4,544,128]{2,1,0:T(8,128)(2,1)} %get-tuple-element.23.refs_1_), channel_id=1, source_target_pairs={{0,2},{2,0},{4,6},{6,4},{8,10},{10,8},{12,14},{14,12},{16,18},{18,... | collective-permute-start | bytes 1671176 | tf_op jit(solution)/shard_map/ppermute | solution.py:442
  19.2 39.1 %collective-permute-start.2 = (bf16[4,544,128]{2,1,0:T(8,128)(2,1)}, bf16[4,544,128]{2,1,0:T(8,128)(2,1)}, u32[]{:S(2)}, u32[]{:S(2)}) collective-permute-start(bf16[4,544,128]{2,1,0:T(8,128)(2,1)} %collective-permute-done.refs_3_), channel_id=1, source_target_pairs={{0,8},{2,10},{4,12},{6,14},{8,16},{10,18},{12,20},{14,22},{16,24},... | collective-permute-start | bytes 1671176 | tf_op jit(solution)/shard_map/ppermute | solution.py:439
  20.5 37.8 %collective-permute-start.3 = (bf16[4,544,128]{2,1,0:T(8,128)(2,1)}, bf16[4,544,128]{2,1,0:T(8,128)(2,1)}, u32[]{:S(2)}, u32[]{:S(2)}) collective-permute-start(bf16[4,544,128]{2,1,0:T(8,128)(2,1)} %collective-permute-done.refs_3_), channel_id=1, source_target_pairs={{0,4},{2,6},{4,0},{6,2},{8,12},{10,14},{12,8},{14,10},{16,20},{18,... | collective-permute-start | bytes 1671176 | tf_op jit(solution)/shard_map/ppermute | solution.py:442
  58.3 17.1 %collective-permute-start.6 = (bf16[4,544,128]{2,1,0:T(8,128)(2,1)}, bf16[4,544,128]{2,1,0:T(8,128)(2,1)}, u32[]{:S(2)}, u32[]{:S(2)}) collective-permute-start(bf16[4,544,128]{2,1,0:T(8,128)(2,1)} %collective-permute-done.2.refs_1_), channel_id=1, source_target_pairs={{0,8},{2,10},{4,12},{6,14},{8,16},{10,18},{12,20},{14,22},{16,24},... | collective-permute-start | bytes 1671176 | tf_op jit(solution)/shard_map/ppermute | solution.py:439
  59.8 54.3 %collective-permute-start.7 = (bf16[4,544,128]{2,1,0:T(8,128)(2,1)}, bf16[4,544,128]{2,1,0:T(8,128)(2,1)}, u32[]{:S(2)}, u32[]{:S(2)}) collective-permute-start(bf16[4,544,128]{2,1,0:T(8,128)(2,1)} %collective-permute-done.2.refs_1_), channel_id=1, source_target_pairs={{0,4},{2,6},{4,0},{6,2},{8,12},{10,14},{12,8},{14,10},{16,20},{18,... | collective-permute-start | bytes 1671176 | tf_op jit(solution)/shard_map/ppermute | solution.py:442
  61.3 53.4 %collective-permute-start.13 = (bf16[4,544,128]{2,1,0:T(8,128)(2,1)}, bf16[4,544,128]{2,1,0:T(8,128)(2,1)}, u32[]{:S(2)}, u32[]{:S(2)}) collective-permute-start(bf16[4,544,128]{2,1,0:T(8,128)(2,1)} %collective-permute-done.refs_3_), channel_id=1, source_target_pairs={{0,2},{2,0},{4,6},{6,4},{8,10},{10,8},{12,14},{14,12},{16,18},{18,... | collective-permute-start | bytes 1671176 | tf_op jit(solution)/shard_map/ppermute | solution.py:442
  61.4 54.6 %collective-permute-start.12 = (bf16[4,544,128]{2,1,0:T(8,128)(2,1)}, bf16[4,544,128]{2,1,0:T(8,128)(2,1)}, u32[]{:S(2)}, u32[]{:S(2)}) collective-permute-start(bf16[4,544,128]{2,1,0:T(8,128)(2,1)} %collective-permute-done.1.refs_1_), channel_id=1, source_target_pairs={{0,2},{2,0},{4,6},{6,4},{8,10},{10,8},{12,14},{14,12},{16,18},{18,... | collective-permute-start | bytes 1671176 | tf_op jit(solution)/shard_map/ppermute | solution.py:442
  61.9 54.5 %collective-permute-start.14 = (bf16[4,544,128]{2,1,0:T(8,128)(2,1)}, bf16[4,544,128]{2,1,0:T(8,128)(2,1)}, u32[]{:S(2)}, u32[]{:S(2)}) collective-permute-start(bf16[4,544,128]{2,1,0:T(8,128)(2,1)} %collective-permute-done.3.refs_5_), channel_id=1, source_target_pairs={{0,2},{2,0},{4,6},{6,4},{8,10},{10,8},{12,14},{14,12},{16,18},{18,... | collective-permute-start | bytes 1671176 | tf_op jit(solution)/shard_map/ppermute | solution.py:442
  75.4 38.8 %collective-permute-start.15 = (f32[1,8,256]{2,1,0:T(8,128)}, f32[1,8,256]{2,1,0:T(8,128)}, u32[]{:S(2)}, u32[]{:S(2)}) collective-permute-start(f32[1,8,256]{2,1,0:T(8,128)} %loss.1.refs_12_), channel_id=1, source_target_pairs={{0,1},{1,0},{2,3},{3,2},{4,5},{5,4},{6,7},{7,6},{8,9},{9,8},{10,11... | collective-permute-start | bytes 24584 | tf_op jit(solution)/shard_map/ppermute | solution.py:462
  114.1 173.2 %collective-permute-start.5 = (bf16[4,544,128]{2,1,0:T(8,128)(2,1)}, bf16[4,544,128]{2,1,0:T(8,128)(2,1)}, u32[]{:S(2)}, u32[]{:S(2)}) collective-permute-start(bf16[4,544,128]{2,1,0:T(8,128)(2,1)} %collective-permute-done.2.refs_1_), channel_id=1, source_target_pairs={{0,2},{2,0},{4,6},{6,4},{8,10},{10,8},{12,14},{14,12},{16,18},{18,... | collective-permute-start | bytes 1671176 | tf_op jit(solution)/shard_map/ppermute | solution.py:442
  114.1 173.1 %collective-permute-start.10 = (bf16[4,544,128]{2,1,0:T(8,128)(2,1)}, bf16[4,544,128]{2,1,0:T(8,128)(2,1)}, u32[]{:S(2)}, u32[]{:S(2)}) collective-permute-start(bf16[4,544,128]{2,1,0:T(8,128)(2,1)} %collective-permute-done.6.refs_5_), channel_id=1, source_target_pairs={{0,4},{2,6},{4,0},{6,2},{8,12},{10,14},{12,8},{14,10},{16,20},{18,... | collective-permute-start | bytes 1671176 | tf_op jit(solution)/shard_map/ppermute | solution.py:442
  114.7 172.6 %collective-permute-start.11 = (bf16[4,544,128]{2,1,0:T(8,128)(2,1)}, bf16[4,544,128]{2,1,0:T(8,128)(2,1)}, u32[]{:S(2)}, u32[]{:S(2)}) collective-permute-start(bf16[4,544,128]{2,1,0:T(8,128)(2,1)} %collective-permute-done.6.refs_5_), channel_id=1, source_target_pairs={{0,6},{2,4},{4,2},{6,0},{8,14},{10,12},{12,10},{14,8},{16,22},{18,... | collective-permute-start | bytes 1671176 | tf_op jit(solution)/shard_map/ppermute | solution.py:442
  116.0 171.3 %collective-permute-start.9 = (bf16[4,544,128]{2,1,0:T(8,128)(2,1)}, bf16[4,544,128]{2,1,0:T(8,128)(2,1)}, u32[]{:S(2)}, u32[]{:S(2)}) collective-permute-start(bf16[4,544,128]{2,1,0:T(8,128)(2,1)} %collective-permute-done.6.refs_5_), channel_id=1, source_target_pairs={{0,2},{2,0},{4,6},{6,4},{8,10},{10,8},{12,14},{14,12},{16,18},{18,... | collective-permute-start | bytes 1671176 | tf_op jit(solution)/shard_map/ppermute | solution.py:442
  116.4 170.9 %collective-permute-start.8 = (bf16[4,544,128]{2,1,0:T(8,128)(2,1)}, bf16[4,544,128]{2,1,0:T(8,128)(2,1)}, u32[]{:S(2)}, u32[]{:S(2)}) collective-permute-start(bf16[4,544,128]{2,1,0:T(8,128)(2,1)} %collective-permute-done.7.refs_3_), channel_id=1, source_target_pairs={{0,2},{2,0},{4,6},{6,4},{8,10},{10,8},{12,14},{14,12},{16,18},{18,... | collective-permute-start | bytes 1671176 | tf_op jit(solution)/shard_map/ppermute | solution.py:442

commit v2 on v1

--- a/solution.py
+++ b/solution.py
@@ -64,6 +64,7 @@
     last = losses > 0
     pairs = len(sources) // 2
     q_ref = refs.pop(0)
+    q_all = q_ref
     blocks = [refs.pop(0) for _ in range(2 * pairs)]
     lst_ref = refs.pop(0)
     if first:
@@ -72,22 +73,23 @@
         acc_in = refs.pop(0)
         top_in = refs.pop(0)
     if chained:
-        refs = refs[2:]
+        refs = refs[3:]
     loss_refs = [refs.pop(0) for _ in range(losses)]
     if last:
-        out_ref, peak_ref, loss_out, acc_out, top_out, q_all, count_ref = refs
+        out_ref, peak_ref, loss_out, acc_out, top_out, count_ref = refs
     elif first:
-        acc_out, top_out, own_s, bias_ref, q_all, count_ref = refs
+        acc_out, top_out, q_all, own_s, bias_ref, count_ref = refs
     else:
-        acc_out, top_out, q_all, count_ref = refs
+        acc_out, top_out, count_ref = refs
     step = pl.program_id(1)
     opening = (pl.program_id(0) == 0) & (step == 0)
     scale = HD ** (-0.5)
     c2 = scale * LOG2E
     chunks = rows // HD
     lead = lst_ref[...] == 0.0
-    for g in range(group):
-        q_all[g] = q_ref[0, :, g * HD : (g + 1) * HD]
+    if first:
+        for g in range(group):
+            q_all[0, g] = q_ref[0, :, g * HD : (g + 1) * HD]
 
     @pl.when(opening)
     def _():
@@ -112,7 +114,7 @@
 
     def values(b):
         parts = [blocks[b][0, rows + h * HD : rows + (h + 1) * HD, :] for h in range(chunks)]
-        return jnp.concatenate(parts, axis=1)
+        return jnp.concatenate([jnp.concatenate(parts, axis=1), jnp.ones((SUB, rows), BF16)], axis=0)
 
     def folded(v, op):
         return op(v.reshape(rows // 8, 8, rows), axis=0)
@@ -131,48 +133,40 @@
             blocks[2 * pair + i][0, 0:rows, :], q, NT, preferred_element_type=F32
         )
 
-    def pair_values(pair):
-        return jnp.concatenate([values(2 * pair), values(2 * pair + 1)], axis=1)
-
-    def visit(chosen, masked, fresh):
+    def pair_values(pair, count=2):
+        return jnp.concatenate([values(2 * pair + i) for i in range(count)], axis=1)
+
+    def visit(chosen, masked, fresh, count=2):
         units = [(g, pair) for g in range(group) for pair in chosen]
-        vts = {pair: pair_values(pair) for pair in chosen}
+        vts = {pair: pair_values(pair, count) for pair in chosen}
         oks = {pair: usable(pair) for pair in chosen} if masked and not first else {}
-        best, sums = {}, {}
+        best = {}
         waiting = []
-        for n in range(len(units) + 2):
+        late = 4 // count
+        for n in range(len(units) + late):
             if n < len(units):
                 g, pair = units[n]
                 probs = []
-                for i in range(2):
-                    s = scores(pair, i, q_all[g])
+                for i in range(count):
+                    s = scores(pair, i, q_all[0, g])
                     if first:
                         s = s + bias_ref[i]
                     elif masked:
                         s = jnp.where(oks[pair][i], s, FILL)
                     m = folded(s, jnp.max)
                     best[g] = jnp.maximum(best[g], m) if g in best else m
-                    p = jnp.exp2(s * c2)
-                    t = folded(p, jnp.sum)
-                    sums[g] = sums[g] + t if g in sums else t
-                    probs.append(p.astype(BF16))
+                    probs.append(jnp.exp2(s * c2).astype(BF16))
                 if pair == chosen[-1]:
                     peak = jnp.max(best.pop(g), axis=0, keepdims=True)
                     if not first:
                         peak = jnp.where(lead, peak, FILL)
                     top_out[0, 1, g : g + 1, :] = jnp.maximum(top_out[0, 1, g : g + 1, :], peak)
                 waiting.append((g, pair, jnp.concatenate(probs, axis=0)))
-            if n >= 2:
+            if n >= late:
                 g, pair, p = waiting.pop(0)
-                more = jnp.dot(vts[pair], p, preferred_element_type=F32)
+                more = jnp.dot(vts[pair], p, preferred_element_type=F32)[0:KEEP]
                 old = acc_in if fresh and pair == chosen[0] else acc_out
-                acc_out[0, g, 0:HD] = old[0, g, 0:HD] + (more if first else jnp.where(lead, more, 0.0))
-                if pair == chosen[-1]:
-                    more = sums.pop(g)
-                    old = acc_in if fresh else acc_out
-                    acc_out[0, g, HD:KEEP] = old[0, g, HD:KEEP] + (
-                        more if first else jnp.where(lead, more, 0.0)
-                    )
+                acc_out[0, g] = old[0, g] + (more if first else jnp.where(lead, more, 0.0))
 
     def revisit(pair):
         ok = usable(pair)
@@ -184,11 +178,10 @@
         def _(g):
             shift = top_out[0, 0, pl.ds(g, 1), :] * c2
             probs = [
-                jnp.exp2(jnp.where(ok[i], scores(pair, i, q_all[g]), FILL) * c2 - shift) for i in range(2)
+                jnp.exp2(jnp.where(ok[i], scores(pair, i, q_all[0, g]), FILL) * c2 - shift) for i in range(2)
             ]
-            acc_out[0, g, HD:KEEP] = acc_out[0, g, HD:KEEP] + sum(folded(p, jnp.sum) for p in probs)
             p = jnp.concatenate(probs, axis=0).astype(BF16)
-            acc_out[0, g, 0:HD] = acc_out[0, g, 0:HD] + jnp.dot(vt, p, preferred_element_type=F32)
+            acc_out[0, g] = acc_out[0, g] + jnp.dot(vt, p, preferred_element_type=F32)[0:KEEP]
 
     if first:
 
@@ -201,7 +194,7 @@
         ones = jnp.ones((SUB, HD), BF16)
 
         def diagonal(g, i):
-            prod = q_all[g].astype(F32) * own_ref[i, 0].astype(F32)
+            prod = q_all[0, g].astype(F32) * own_ref[i, 0].astype(F32)
             high = prod.astype(BF16)
             low = (prod - high.astype(F32)).astype(BF16)
             both = jnp.concatenate([high, low], axis=1)
@@ -227,7 +220,7 @@
             for g in range(group):
                 acc_out[0, g, 0:HD] = jnp.zeros((HD, rows), F32)
                 acc_out[0, g, HD:KEEP] = jnp.broadcast_to(
-                    functools.reduce(jnp.add, weights)[g : g + 1, :] * (1.0 / (KEEP - HD)), (KEEP - HD, rows)
+                    functools.reduce(jnp.add, weights)[g : g + 1, :], (KEEP - HD, rows)
                 )
             for i in range(1, steps):
 
@@ -239,7 +232,15 @@
                         acc_out[0, g, 0:HD] = acc_out[0, g, 0:HD] + own_val * w
 
         start()
-        visit([0], True, False)
+
+        @pl.when(count_ref[1] < rows)
+        def _():
+            visit([0], True, False)
+
+        @pl.when(count_ref[1] >= rows)
+        def _():
+            visit([0], True, False, 1)
+
         spread = jnp.max(jnp.abs(top_out[0, 1])) * c2
 
         @pl.when(spread > LIMIT)
@@ -269,9 +270,26 @@
 
         for pair in range(pairs):
 
-            @pl.when(some[pair] & jnp.logical_not(all_full & (pair in joined)))
+            alone = some[pair] & jnp.logical_not(all_full & (pair in joined))
+            plain = full[pair] if last and pair not in joined else False
+
+            half = (count_ref[2 * pair + 1] >= rows) if last else False
+
+            @pl.when(alone & jnp.logical_not(plain) & jnp.logical_not(half))
             def _():
                 visit([pair], True, False)
+
+            if last:
+
+                @pl.when(alone & half)
+                def _():
+                    visit([pair], True, False, 1)
+
+            if last and pair not in joined:
+
+                @pl.when(alone & plain)
+                def _():
+                    visit([pair], False, False)
 
         past = top_in[0, 0]
         spread = jnp.maximum(jnp.max(top_out[0, 1]) * c2 - LIMIT, jnp.max(jnp.abs(past)))
@@ -290,8 +308,8 @@
 
     if last:
         for g in range(group):
-            o = acc_out[0, g, 0:HD] * (1.0 / jnp.sum(acc_out[0, g, HD:KEEP], axis=0, keepdims=True))
-            out_ref[0, :, g * HD : (g + 1) * HD] = o.T.astype(BF16)
+            o = acc_out[0, g, 0:HD] * (1.0 / acc_out[0, g, HD : HD + 1])
+            out_ref[0, :, g * HD : (g + 1) * HD] = o.astype(BF16).T
         peak_ref[0] = top_out[0, 1] * scale
 
 
@@ -309,20 +327,23 @@
     acc_spec = pl.BlockSpec((1, group, KEEP, rows), lambda k, j, s: ((k + low) * steps + j, 0, 0, 0))
     top_spec = pl.BlockSpec((1, 2, group, rows), lambda k, j, s: ((k + low) * steps + j, 0, 0, 0))
     row_spec = pl.BlockSpec((1, rows), lambda k, j, s: (0, 0))
+    wide_spec = pl.BlockSpec((1, rows, group * HD), lambda k, j, s: (j, 0, k + low))
+    tile_spec = pl.BlockSpec((1, group, rows, HD), lambda k, j, s: ((k + low) * steps + j, 0, 0, 0))
     in_specs = (
-        [pl.BlockSpec((1, rows, group * HD), lambda k, j, s: (j, 0, k + low))]
+        [wide_spec if first else tile_spec]
         + [pl.BlockSpec((1, depth, HD), lambda k, j, s: (k + low, 0, 0))] * len(blocks)
         + [row_spec]
     )
-    args = [queries] + blocks + [lstart]
+    args = [queries if first else state[2]] + blocks + [lstart]
     scratch = [
-        pltpu.VMEM((group, rows, HD), BF16),
         pltpu.SMEM((len(blocks),), jnp.int32),
     ]
     aliases = {}
     out_shape = [jax.ShapeDtypeStruct(acc_shape, F32), jax.ShapeDtypeStruct(top_shape, F32)]
     out_specs = [acc_spec, top_spec]
     if first:
+        out_shape += [jax.ShapeDtypeStruct((kvl * steps, group, rows, HD), BF16)]
+        out_specs += [tile_spec]
         args += [draft_kv]
         in_specs += [pl.BlockSpec((steps, 2, rows, HD), lambda k, j, s: (0, 0, 0, k + low))]
         scratch = [
@@ -331,8 +352,10 @@
         ] + scratch
     if state is not None:
         aliases = {len(args) + 1: 0, len(args) + 2: 1}
-        args += list(state)
-        in_specs += [pl.BlockSpec(memory_space=pl.ANY)] * 2 if first else [acc_spec, top_spec]
+        if first:
+            aliases[len(args) + 3] = 2
+        args += state[: 3 if first else 2]
+        in_specs += [pl.BlockSpec(memory_space=pl.ANY)] * 3 if first else [acc_spec, top_spec]
     if last:
         aliases = {}
         args += losses
@@ -477,7 +500,7 @@
         level = len(c)
         if level < levels:
             z[level], x[level - 1], top = lax.optimization_barrier((z[level], x[level - 1], state[1]))
-            state = [state[0], top]
+            state = [state[0], top, state[2]]
             spread(level)
     while len(c) < levels:
         spread(len(c))
@@ -487,7 +510,8 @@
     split = [0, 6] + list(range(14, len(rest) + 1, 8))
     for begin, end in zip(split, split[1:]):
         final = end == len(rest)
-        state = run(rest[begin:end], state, losses=losses if final else [])
+        moved = run(rest[begin:end], state, losses=losses if final else [])
+        state = moved if final else [*moved, state[2]]
     out, peaks, token_loss = state
     return (out, peaks.transpose(0, 2, 1), token_loss.reshape(-1))
 

time: 467 us -> 462 us (0.989)
  Pallas kernels: 438 us -> 430 us
    pallas_call x4, Pallas kernels: 424 us -> 415 us  [stage(): pl.pallas_call(functools.partial(stage_kernel, group, rows, steps, source...]
where the time goes in v2:
time: 462 us; the launch traced here: 461 us
  Pallas kernels  430 us (93%)
  waiting for transfers between devices  15.9 us (3%)
  starting transfers between devices  14.1 us (3%)
    pallas_call x4, Pallas kernels, stage(): pl.pallas_call(functools.partial(stage_kernel, group, rows, steps, source...  415 us
    ppermute x3, waiting for transfers between devices, up(): return lax.ppermute(x, 'seq', [(i, i + 4) for i in range(shards - 4)])  15.9 us
    pallas_call x1, Pallas kernels, loss_parts(): pl.pallas_call(functools.partial(loss_kernel, block, width), grid_spec=pl...  12.2 us
  transfers between devices with their start and end apart: 16, of which 2 were waited for; matrix products, arithmetic and copies ran while one was open for 0% of the time, Pallas kernels for 55%

profile of v2, /device:TPU:26, one launch (start us, length us, event | category | flops | bytes accessed | tf_op | source)
XLA Modules:
  0.0 460.7 jit_solution(8306958174305563279)
XLA Ops:
  0.6 2.0 pack.1
  2.7 1.3 collective-permute-start.1
  4.0 0.6 collective-permute-start.2
  4.6 0.0 collective-permute-start
  4.6 12.2 %loss.1.refs_12_ = f32[1,8,256]{2,1,0:T(8,128)} custom-call(s32[256]{0:T(256)} %tgt_ref.1, bf16[256,32768]{1,0:T(8,128)(2,1)} %x_ref.1), custom_call_target="tpu_custom_call" | custom-call | flops 33554432 | bytes 16777216 | tf_op jit(solution)/shard_map/loss/pallas_call | solution.py:438
  16.8 2.4 collective-permute-done.1.refs_3_
  19.2 0.0 collective-permute-done.2.refs_1_
  19.2 1.3 collective-permute-start.3
  20.5 0.6 collective-permute-start.4
  21.1 0.0 collective-permute-done.refs_2_
  21.1 35.5 %stage_first.2 = (f32[12,8,136,256]{3,2,1,0:T(8,128)}, f32[12,2,8,256]{3,2,1,0:T(8,128)}, bf16[12,8,256,128]{3,2,1,0:T(8,128)(2,1)}) custom-call(s32[256]{0:T(256)} %doc_ref.7, bf16[3,256,4096]{2,1,0:T(8,128)(2,1)} %refs_0_.3, bf16[4,544,128]{2,1,0:T(8,128)(2,1)} %get-tuple-element.25.refs_1_, bf16[4,544,128]{2,1,0:T(8,128)(2,1)} %collective-permute-done.refs_2_, ...), custom_call_target="tpu_custom_call" | custom-call | flops 3221225472 | bytes 12582912 | tf_op jit(solution)/shard_map/stage_first/pallas_call | solution.py:378
  56.6 0.0 collective-permute-done.3.refs_1_
  56.6 0.0 collective-permute-done.4.refs_5_
  56.6 1.5 collective-permute-start.6
  58.1 1.6 collective-permute-start.7
  59.6 0.5 collective-permute-start.13
  60.2 0.0 collective-permute-start.12
  60.2 0.5 collective-permute-start.14
  60.7 13.4 %collective-permute-done.6.refs_5_ = bf16[4,544,128]{2,1,0:T(8,128)(2,1)} collective-permute-done((bf16[4,544,128]{2,1,0:T(8,128)(2,1)}, bf16[4,544,128]{2,1,0:T(8,128)(2,1)}, u32[]{:S(2)}, u32[]{:S(2)}) %collective-permute-start.6) | collective-permute-done | bytes 557088 | tf_op jit(solution)/shard_map/ppermute | solution.py:462
  74.1 1.5 collective-permute-start.15
  75.6 35.5 %stage_first.3 = (f32[12,8,136,256]{3,2,1,0:T(8,128)}, f32[12,2,8,256]{3,2,1,0:T(8,128)}, bf16[12,8,256,128]{3,2,1,0:T(8,128)(2,1)}) custom-call(s32[256]{0:T(256)} %doc_ref.7, bf16[3,256,4096]{2,1,0:T(8,128)(2,1)} %refs_0_.3, bf16[4,544,128]{2,1,0:T(8,128)(2,1)} %get-tuple-element.25.refs_1_, ...), custom_call_target="tpu_custom_call", output_to_operand_aliasing={{0}: (6, {}), {1}: (7, {}), {2}: (8, {})} | custom-call | flops 3221225472 | bytes 12582912 | tf_op jit(solution)/shard_map/stage_first/pallas_call | solution.py:378
  111.2 0.0 collective-permute-done.7.refs_3_
  111.2 2.6 collective-permute-start.5
  113.7 0.0 collective-permute-done.15.refs_13_
  113.7 1.5 collective-permute-start.10
  115.3 0.0 collective-permute-done.13.refs_4_
  115.3 0.0 collective-permute-start.11
  115.3 0.0 collective-permute-done.12.refs_2_
  115.3 0.6 collective-permute-start.9
  115.9 0.0 collective-permute-done.14.refs_6_
  115.9 0.1 collective-permute-start.8
  116.0 168.6 %stage_mid.1 = (f32[12,8,136,256]{3,2,1,0:T(8,128)}, f32[12,2,8,256]{3,2,1,0:T(8,128)}) custom-call(s32[256]{0:T(256)} %doc_ref.7, bf16[12,8,256,128]{3,2,1,0:T(8,128)(2,1)} %get-tuple-element.32.refs_0_, bf16[4,544,128]{2,1,0:T(8,128)(2,1)} %collective-permute-done.2.refs_1_, ...), custom_call_target="tpu_custom_call", output_to_operand_aliasing={{0}: (9, {}), {1}: (10, {})} | custom-call | flops 19327352832 | bytes 12582912 | tf_op jit(solution)/shard_map/stage_mid/pallas_call | solution.py:378
  284.5 0.0 collective-permute-done.5.refs_2_
  284.6 0.0 collective-permute-done.10.refs_7_
  284.6 0.0 collective-permute-done.11.refs_8_
  284.6 0.0 collective-permute-done.8.refs_4_
  284.6 0.0 collective-permute-done.9.refs_6_
  284.6 175.9 %stage_last.1 = (bf16[3,256,4096]{2,1,0:T(8,128)(2,1)}, f32[3,32,256]{2,1,0:T(8,128)}, f32[1,256]{1,0:T(1,128)}) custom-call(s32[256]{0:T(256)} %doc_ref.7, bf16[12,8,256,128]{3,2,1,0:T(8,128)(2,1)} %get-tuple-element.32.refs_0_, bf16[4,544,128]{2,1,0:T(8,128)(2,1)} %collective-permute-done.3.refs_1_, bf16[4,544,128]{2,1,0:T(8,128)(2,1)} %collective-permute-done.5.refs_2_, ...), custom_call_target="tpu_custom_call" | custom-call | flops 25769803776 | bytes 12582912 | tf_op jit(solution)/shard_map/stage_last/pallas_call | solution.py:378
Async XLA Ops:
  2.7 16.6 %collective-permute-start.1 = (bf16[4,544,128]{2,1,0:T(8,128)(2,1)}, bf16[4,544,128]{2,1,0:T(8,128)(2,1)}, u32[]{:S(2)}, u32[]{:S(2)}) collective-permute-start(bf16[4,544,128]{2,1,0:T(8,128)(2,1)} %get-tuple-element.25.refs_1_), channel_id=1, source_target_pairs={{0,8},{2,10},{4,12},{6,14},{8,16},{10,18},{12,20},{14,22},{16,24},... | collective-permute-start | bytes 1671176 | tf_op jit(solution)/shard_map/ppermute | solution.py:462
  4.0 15.3 %collective-permute-start.2 = (bf16[4,544,128]{2,1,0:T(8,128)(2,1)}, bf16[4,544,128]{2,1,0:T(8,128)(2,1)}, u32[]{:S(2)}, u32[]{:S(2)}) collective-permute-start(bf16[4,544,128]{2,1,0:T(8,128)(2,1)} %get-tuple-element.25.refs_1_), channel_id=1, source_target_pairs={{0,4},{2,6},{4,0},{6,2},{8,12},{10,14},{12,8},{14,10},{16,20},{18,... | collective-permute-start | bytes 1671176 | tf_op jit(solution)/shard_map/ppermute | solution.py:465
  4.6 16.6 %collective-permute-start = (bf16[4,544,128]{2,1,0:T(8,128)(2,1)}, bf16[4,544,128]{2,1,0:T(8,128)(2,1)}, u32[]{:S(2)}, u32[]{:S(2)}) collective-permute-start(bf16[4,544,128]{2,1,0:T(8,128)(2,1)} %get-tuple-element.25.refs_1_), channel_id=1, source_target_pairs={{0,2},{2,0},{4,6},{6,4},{8,10},{10,8},{12,14},{14,12},{16,18},{18,... | collective-permute-start | bytes 1671176 | tf_op jit(solution)/shard_map/ppermute | solution.py:465
  19.2 37.3 %collective-permute-start.3 = (bf16[4,544,128]{2,1,0:T(8,128)(2,1)}, bf16[4,544,128]{2,1,0:T(8,128)(2,1)}, u32[]{:S(2)}, u32[]{:S(2)}) collective-permute-start(bf16[4,544,128]{2,1,0:T(8,128)(2,1)} %collective-permute-done.1.refs_3_), channel_id=1, source_target_pairs={{0,8},{2,10},{4,12},{6,14},{8,16},{10,18},{12,20},{14,22},{16,24},... | collective-permute-start | bytes 1671176 | tf_op jit(solution)/shard_map/ppermute | solution.py:462
  20.5 36.1 %collective-permute-start.4 = (bf16[4,544,128]{2,1,0:T(8,128)(2,1)}, bf16[4,544,128]{2,1,0:T(8,128)(2,1)}, u32[]{:S(2)}, u32[]{:S(2)}) collective-permute-start(bf16[4,544,128]{2,1,0:T(8,128)(2,1)} %collective-permute-done.1.refs_3_), channel_id=1, source_target_pairs={{0,4},{2,6},{4,0},{6,2},{8,12},{10,14},{12,8},{14,10},{16,20},{18,... | collective-permute-start | bytes 1671176 | tf_op jit(solution)/shard_map/ppermute | solution.py:465
  56.6 17.5 %collective-permute-start.6 = (bf16[4,544,128]{2,1,0:T(8,128)(2,1)}, bf16[4,544,128]{2,1,0:T(8,128)(2,1)}, u32[]{:S(2)}, u32[]{:S(2)}) collective-permute-start(bf16[4,544,128]{2,1,0:T(8,128)(2,1)} %collective-permute-done.3.refs_1_), channel_id=1, source_target_pairs={{0,8},{2,10},{4,12},{6,14},{8,16},{10,18},{12,20},{14,22},{16,24},... | collective-permute-start | bytes 1671176 | tf_op jit(solution)/shard_map/ppermute | solution.py:462
  58.1 53.1 %collective-permute-start.7 = (bf16[4,544,128]{2,1,0:T(8,128)(2,1)}, bf16[4,544,128]{2,1,0:T(8,128)(2,1)}, u32[]{:S(2)}, u32[]{:S(2)}) collective-permute-start(bf16[4,544,128]{2,1,0:T(8,128)(2,1)} %collective-permute-done.3.refs_1_), channel_id=1, source_target_pairs={{0,4},{2,6},{4,0},{6,2},{8,12},{10,14},{12,8},{14,10},{16,20},{18,... | collective-permute-start | bytes 1671176 | tf_op jit(solution)/shard_map/ppermute | solution.py:465
  59.6 55.6 %collective-permute-start.13 = (bf16[4,544,128]{2,1,0:T(8,128)(2,1)}, bf16[4,544,128]{2,1,0:T(8,128)(2,1)}, u32[]{:S(2)}, u32[]{:S(2)}) collective-permute-start(bf16[4,544,128]{2,1,0:T(8,128)(2,1)} %collective-permute-done.1.refs_3_), channel_id=1, source_target_pairs={{0,2},{2,0},{4,6},{6,4},{8,10},{10,8},{12,14},{14,12},{16,18},{18,... | collective-permute-start | bytes 1671176 | tf_op jit(solution)/shard_map/ppermute | solution.py:465
  60.2 55.1 %collective-permute-start.12 = (bf16[4,544,128]{2,1,0:T(8,128)(2,1)}, bf16[4,544,128]{2,1,0:T(8,128)(2,1)}, u32[]{:S(2)}, u32[]{:S(2)}) collective-permute-start(bf16[4,544,128]{2,1,0:T(8,128)(2,1)} %collective-permute-done.2.refs_1_), channel_id=1, source_target_pairs={{0,2},{2,0},{4,6},{6,4},{8,10},{10,8},{12,14},{14,12},{16,18},{18,... | collective-permute-start | bytes 1671176 | tf_op jit(solution)/shard_map/ppermute | solution.py:465
  60.2 55.7 %collective-permute-start.14 = (bf16[4,544,128]{2,1,0:T(8,128)(2,1)}, bf16[4,544,128]{2,1,0:T(8,128)(2,1)}, u32[]{:S(2)}, u32[]{:S(2)}) collective-permute-start(bf16[4,544,128]{2,1,0:T(8,128)(2,1)} %collective-permute-done.4.refs_5_), channel_id=1, source_target_pairs={{0,2},{2,0},{4,6},{6,4},{8,10},{10,8},{12,14},{14,12},{16,18},{18,... | collective-permute-start | bytes 1671176 | tf_op jit(solution)/shard_map/ppermute | solution.py:465
  74.1 39.6 %collective-permute-start.15 = (f32[1,8,256]{2,1,0:T(8,128)}, f32[1,8,256]{2,1,0:T(8,128)}, u32[]{:S(2)}, u32[]{:S(2)}) collective-permute-start(f32[1,8,256]{2,1,0:T(8,128)} %loss.1.refs_12_), channel_id=1, source_target_pairs={{0,1},{1,0},{2,3},{3,2},{4,5},{5,4},{6,7},{7,6},{8,9},{9,8},{10,11... | collective-permute-start | bytes 24584 | tf_op jit(solution)/shard_map/ppermute | solution.py:485
  111.2 173.4 %collective-permute-start.5 = (bf16[4,544,128]{2,1,0:T(8,128)(2,1)}, bf16[4,544,128]{2,1,0:T(8,128)(2,1)}, u32[]{:S(2)}, u32[]{:S(2)}) collective-permute-start(bf16[4,544,128]{2,1,0:T(8,128)(2,1)} %collective-permute-done.3.refs_1_), channel_id=1, source_target_pairs={{0,2},{2,0},{4,6},{6,4},{8,10},{10,8},{12,14},{14,12},{16,18},{18,... | collective-permute-start | bytes 1671176 | tf_op jit(solution)/shard_map/ppermute | solution.py:465
  113.7 170.8 %collective-permute-start.10 = (bf16[4,544,128]{2,1,0:T(8,128)(2,1)}, bf16[4,544,128]{2,1,0:T(8,128)(2,1)}, u32[]{:S(2)}, u32[]{:S(2)}) collective-permute-start(bf16[4,544,128]{2,1,0:T(8,128)(2,1)} %collective-permute-done.6.refs_5_), channel_id=1, source_target_pairs={{0,4},{2,6},{4,0},{6,2},{8,12},{10,14},{12,8},{14,10},{16,20},{18,... | collective-permute-start | bytes 1671176 | tf_op jit(solution)/shard_map/ppermute | solution.py:465
  115.3 169.3 %collective-permute-start.11 = (bf16[4,544,128]{2,1,0:T(8,128)(2,1)}, bf16[4,544,128]{2,1,0:T(8,128)(2,1)}, u32[]{:S(2)}, u32[]{:S(2)}) collective-permute-start(bf16[4,544,128]{2,1,0:T(8,128)(2,1)} %collective-permute-done.6.refs_5_), channel_id=1, source_target_pairs={{0,6},{2,4},{4,2},{6,0},{8,14},{10,12},{12,10},{14,8},{16,22},{18,... | collective-permute-start | bytes 1671176 | tf_op jit(solution)/shard_map/ppermute | solution.py:465
  115.3 169.3 %collective-permute-start.9 = (bf16[4,544,128]{2,1,0:T(8,128)(2,1)}, bf16[4,544,128]{2,1,0:T(8,128)(2,1)}, u32[]{:S(2)}, u32[]{:S(2)}) collective-permute-start(bf16[4,544,128]{2,1,0:T(8,128)(2,1)} %collective-permute-done.6.refs_5_), channel_id=1, source_target_pairs={{0,2},{2,0},{4,6},{6,4},{8,10},{10,8},{12,14},{14,12},{16,18},{18,... | collective-permute-start | bytes 1671176 | tf_op jit(solution)/shard_map/ppermute | solution.py:465
  115.9 168.7 %collective-permute-start.8 = (bf16[4,544,128]{2,1,0:T(8,128)(2,1)}, bf16[4,544,128]{2,1,0:T(8,128)(2,1)}, u32[]{:S(2)}, u32[]{:S(2)}) collective-permute-start(bf16[4,544,128]{2,1,0:T(8,128)(2,1)} %collective-permute-done.7.refs_3_), channel_id=1, source_target_pairs={{0,2},{2,0},{4,6},{6,4},{8,10},{10,8},{12,14},{14,12},{16,18},{18,... | collective-permute-start | bytes 1671176 | tf_op jit(solution)/shard_map/ppermute | solution.py:465

commit v3 on v2

--- a/solution.py
+++ b/solution.py
@@ -76,11 +76,11 @@
         refs = refs[3:]
     loss_refs = [refs.pop(0) for _ in range(losses)]
     if last:
-        out_ref, peak_ref, loss_out, acc_out, top_out, count_ref = refs
+        out_ref, peak_ref, loss_out, acc_out, top_out, bias_ref, count_ref = refs
     elif first:
         acc_out, top_out, q_all, own_s, bias_ref, count_ref = refs
     else:
-        acc_out, top_out, count_ref = refs
+        acc_out, top_out, bias_ref, count_ref = refs
     step = pl.program_id(1)
     opening = (pl.program_id(0) == 0) & (step == 0)
     scale = HD ** (-0.5)
@@ -139,7 +139,6 @@
     def visit(chosen, masked, fresh, count=2):
         units = [(g, pair) for g in range(group) for pair in chosen]
         vts = {pair: pair_values(pair, count) for pair in chosen}
-        oks = {pair: usable(pair) for pair in chosen} if masked and not first else {}
         best = {}
         waiting = []
         late = 4 // count
@@ -149,10 +148,8 @@
                 probs = []
                 for i in range(count):
                     s = scores(pair, i, q_all[0, g])
-                    if first:
-                        s = s + bias_ref[i]
-                    elif masked:
-                        s = jnp.where(oks[pair][i], s, FILL)
+                    if masked:
+                        s = s + bias_ref[2 * pair + i]
                     m = folded(s, jnp.max)
                     best[g] = jnp.maximum(best[g], m) if g in best else m
                     probs.append(jnp.exp2(s * c2).astype(BF16))
@@ -183,13 +180,13 @@
             p = jnp.concatenate(probs, axis=0).astype(BF16)
             acc_out[0, g] = acc_out[0, g] + jnp.dot(vt, p, preferred_element_type=F32)[0:KEEP]
 
+    @pl.when(opening)
+    def _():
+        for pair in range(pairs):
+            for i, ok in enumerate(usable(pair)):
+                bias_ref[2 * pair + i] = jnp.where(ok, 0.0, FILL)
+
     if first:
-
-        @pl.when(opening)
-        def _():
-            for i, ok in enumerate(usable(0)):
-                bias_ref[i] = jnp.where(ok, 0.0, FILL)
-
 
         ones = jnp.ones((SUB, HD), BF16)
 
@@ -256,40 +253,40 @@
             a, b = count_ref[2 * pair], count_ref[2 * pair + 1]
             some.append(jnp.minimum(a, b) < rows)
             full.append(jnp.maximum(a, b) == 0)
-        joined = list(range(2 if last else pairs))
-        all_full = functools.reduce(jnp.logical_and, [full[pair] for pair in joined])
-
-        @pl.when(all_full)
-        def _():
-            visit(joined, False, True)
-
-        @pl.when(jnp.logical_not(all_full))
-        def _():
-            for g in range(group):
-                acc_out[0, g] = acc_in[0, g]
+        half = [count_ref[2 * pair + 1] >= rows for pair in range(pairs)]
+
+        together = {}
+        for begin in range(pairs % 2, pairs, 2):
+            a, b = begin, begin + 1
+            plain = begin < 2
+            if plain:
+                both = full[a] & full[b]
+            else:
+                both = some[a] & some[b] & jnp.logical_not(half[a] | half[b])
+            together[a] = together[b] = both
+            opens = begin < 2
+
+            @pl.when(both)
+            def _():
+                visit([a, b], not plain, opens)
+
+            if opens:
+
+                @pl.when(jnp.logical_not(both))
+                def _():
+                    for g in range(group):
+                        acc_out[0, g] = acc_in[0, g]
 
         for pair in range(pairs):
-
-            alone = some[pair] & jnp.logical_not(all_full & (pair in joined))
-            plain = full[pair] if last and pair not in joined else False
-
-            half = (count_ref[2 * pair + 1] >= rows) if last else False
-
-            @pl.when(alone & jnp.logical_not(plain) & jnp.logical_not(half))
+            alone = some[pair] & jnp.logical_not(together.get(pair, False))
+
+            @pl.when(alone & jnp.logical_not(half[pair]))
             def _():
                 visit([pair], True, False)
 
-            if last:
-
-                @pl.when(alone & half)
-                def _():
-                    visit([pair], True, False, 1)
-
-            if last and pair not in joined:
-
-                @pl.when(alone & plain)
-                def _():
-                    visit([pair], False, False)
+            @pl.when(alone & half[pair])
+            def _():
+                visit([pair], True, False, 1)
 
         past = top_in[0, 0]
         spread = jnp.maximum(jnp.max(top_out[0, 1]) * c2 - LIMIT, jnp.max(jnp.abs(past)))
@@ -336,6 +333,7 @@
     )
     args = [queries if first else state[2]] + blocks + [lstart]
     scratch = [
+        pltpu.VMEM((len(blocks), rows, rows), F32),
         pltpu.SMEM((len(blocks),), jnp.int32),
     ]
     aliases = {}
@@ -348,7 +346,6 @@
         in_specs += [pl.BlockSpec((steps, 2, rows, HD), lambda k, j, s: (0, 0, 0, k + low))]
         scratch = [
             pltpu.VMEM((steps, group, rows), F32),
-            pltpu.VMEM((2, rows, rows), F32),
         ] + scratch
     if state is not None:
         aliases = {len(args) + 1: 0, len(args) + 2: 1}
@@ -376,7 +373,9 @@
         ] + scratch
     work = (high - low) * steps * group * rows * rows * len(blocks)
     return pl.pallas_call(
-        functools.partial(stage_kernel, group, rows, steps, sources, first, chained, len(losses)),
+        functools.partial(
+            stage_kernel, group, rows, steps, sources, first, chained, len(losses)
+        ),
         out_shape=out_shape,
         grid_spec=pltpu.PrefetchScalarGridSpec(
             num_scalar_prefetch=1,

time: 462 us -> 464 us (level)
  no operation moved by 1% of the time
where the time goes in v3:
time: 464 us; the launch traced here: 463 us
  Pallas kernels  432 us (93%)
  waiting for transfers between devices  16.1 us (3%)
  starting transfers between devices  14 us (3%)
    pallas_call x4, Pallas kernels, stage(): pl.pallas_call(functools.partial(stage_kernel, group, rows, steps, source...  418 us
    ppermute x3, waiting for transfers between devices, up(): return lax.ppermute(x, 'seq', [(i, i + 4) for i in range(shards - 4)])  16 us
    pallas_call x1, Pallas kernels, loss_parts(): pl.pallas_call(functools.partial(loss_kernel, block, width), grid_spec=pl...  12.2 us
  transfers between devices with their start and end apart: 16, of which 2 were waited for; matrix products, arithmetic and copies ran while one was open for 0% of the time, Pallas kernels for 55%

profile of v3, /device:TPU:26, one launch (start us, length us, event | category | flops | bytes accessed | tf_op | source)
XLA Modules:
  0.0 462.7 jit_solution(1215186309324266075)
XLA Ops:
  0.6 2.0 pack.1
  2.7 1.3 collective-permute-start.1
  4.0 0.6 collective-permute-start.2
  4.6 0.0 collective-permute-start
  4.6 12.2 %loss.1.refs_12_ = f32[1,8,256]{2,1,0:T(8,128)} custom-call(s32[256]{0:T(256)} %tgt_ref.1, bf16[256,32768]{1,0:T(8,128)(2,1)} %x_ref.1), custom_call_target="tpu_custom_call" | custom-call | flops 33554432 | bytes 16777216 | tf_op jit(solution)/shard_map/loss/pallas_call | solution.py:437
  16.8 2.4 collective-permute-done.1.refs_3_
  19.2 0.0 collective-permute-done.2.refs_1_
  19.2 1.3 collective-permute-start.3
  20.5 0.6 collective-permute-start.4
  21.1 0.0 collective-permute-done.refs_2_
  21.1 35.5 %stage_first.2 = (f32[12,8,136,256]{3,2,1,0:T(8,128)}, f32[12,2,8,256]{3,2,1,0:T(8,128)}, bf16[12,8,256,128]{3,2,1,0:T(8,128)(2,1)}) custom-call(s32[256]{0:T(256)} %doc_ref.7, bf16[3,256,4096]{2,1,0:T(8,128)(2,1)} %refs_0_.3, bf16[4,544,128]{2,1,0:T(8,128)(2,1)} %get-tuple-element.25.refs_1_, bf16[4,544,128]{2,1,0:T(8,128)(2,1)} %collective-permute-done.refs_2_, ...), custom_call_target="tpu_custom_call" | custom-call | flops 3221225472 | bytes 12582912 | tf_op jit(solution)/shard_map/stage_first/pallas_call | solution.py:375
  56.6 0.0 collective-permute-done.3.refs_1_
  56.6 0.0 collective-permute-done.4.refs_5_
  56.6 1.3 collective-permute-start.6
  57.9 1.6 collective-permute-start.7
  59.5 0.5 collective-permute-start.13
  60.0 0.0 collective-permute-start.12
  60.0 0.5 collective-permute-start.14
  60.5 13.6 %collective-permute-done.6.refs_5_ = bf16[4,544,128]{2,1,0:T(8,128)(2,1)} collective-permute-done((bf16[4,544,128]{2,1,0:T(8,128)(2,1)}, bf16[4,544,128]{2,1,0:T(8,128)(2,1)}, u32[]{:S(2)}, u32[]{:S(2)}) %collective-permute-start.6) | collective-permute-done | bytes 557088 | tf_op jit(solution)/shard_map/ppermute | solution.py:461
  74.1 1.5 collective-permute-start.15
  75.6 35.7 %stage_first.3 = (f32[12,8,136,256]{3,2,1,0:T(8,128)}, f32[12,2,8,256]{3,2,1,0:T(8,128)}, bf16[12,8,256,128]{3,2,1,0:T(8,128)(2,1)}) custom-call(s32[256]{0:T(256)} %doc_ref.7, bf16[3,256,4096]{2,1,0:T(8,128)(2,1)} %refs_0_.3, bf16[4,544,128]{2,1,0:T(8,128)(2,1)} %get-tuple-element.25.refs_1_, ...), custom_call_target="tpu_custom_call", output_to_operand_aliasing={{0}: (6, {}), {1}: (7, {}), {2}: (8, {})} | custom-call | flops 3221225472 | bytes 12582912 | tf_op jit(solution)/shard_map/stage_first/pallas_call | solution.py:375
  111.3 0.0 collective-permute-done.7.refs_3_
  111.3 2.6 collective-permute-start.5
  113.9 0.0 collective-permute-done.15.refs_13_
  113.9 1.5 collective-permute-start.10
  115.4 0.0 collective-permute-done.13.refs_4_
  115.4 0.0 collective-permute-start.11
  115.4 0.0 collective-permute-done.12.refs_2_
  115.4 0.6 collective-permute-start.9
  116.1 0.0 collective-permute-done.14.refs_6_
  116.1 0.1 collective-permute-start.8
  116.1 171.7 %stage_mid.1 = (f32[12,8,136,256]{3,2,1,0:T(8,128)}, f32[12,2,8,256]{3,2,1,0:T(8,128)}) custom-call(s32[256]{0:T(256)} %doc_ref.7, bf16[12,8,256,128]{3,2,1,0:T(8,128)(2,1)} %get-tuple-element.32.refs_0_, bf16[4,544,128]{2,1,0:T(8,128)(2,1)} %collective-permute-done.2.refs_1_, ...), custom_call_target="tpu_custom_call", output_to_operand_aliasing={{0}: (9, {}), {1}: (10, {})} | custom-call | flops 19327352832 | bytes 12582912 | tf_op jit(solution)/shard_map/stage_mid/pallas_call | solution.py:375
  287.8 0.0 collective-permute-done.5.refs_2_
  287.8 0.0 collective-permute-done.10.refs_7_
  287.8 0.0 collective-permute-done.11.refs_8_
  287.8 0.0 collective-permute-done.8.refs_4_
  287.9 0.0 collective-permute-done.9.refs_6_
  287.9 174.7 %stage_last.1 = (bf16[3,256,4096]{2,1,0:T(8,128)(2,1)}, f32[3,32,256]{2,1,0:T(8,128)}, f32[1,256]{1,0:T(1,128)}) custom-call(s32[256]{0:T(256)} %doc_ref.7, bf16[12,8,256,128]{3,2,1,0:T(8,128)(2,1)} %get-tuple-element.32.refs_0_, bf16[4,544,128]{2,1,0:T(8,128)(2,1)} %collective-permute-done.3.refs_1_, bf16[4,544,128]{2,1,0:T(8,128)(2,1)} %collective-permute-done.5.refs_2_, ...), custom_call_target="tpu_custom_call" | custom-call | flops 25769803776 | bytes 12582912 | tf_op jit(solution)/shard_map/stage_last/pallas_call | solution.py:375
Async XLA Ops:
  2.7 16.6 %collective-permute-start.1 = (bf16[4,544,128]{2,1,0:T(8,128)(2,1)}, bf16[4,544,128]{2,1,0:T(8,128)(2,1)}, u32[]{:S(2)}, u32[]{:S(2)}) collective-permute-start(bf16[4,544,128]{2,1,0:T(8,128)(2,1)} %get-tuple-element.25.refs_1_), channel_id=1, source_target_pairs={{0,8},{2,10},{4,12},{6,14},{8,16},{10,18},{12,20},{14,22},{16,24},... | collective-permute-start | bytes 1671176 | tf_op jit(solution)/shard_map/ppermute | solution.py:461
  4.0 15.3 %collective-permute-start.2 = (bf16[4,544,128]{2,1,0:T(8,128)(2,1)}, bf16[4,544,128]{2,1,0:T(8,128)(2,1)}, u32[]{:S(2)}, u32[]{:S(2)}) collective-permute-start(bf16[4,544,128]{2,1,0:T(8,128)(2,1)} %get-tuple-element.25.refs_1_), channel_id=1, source_target_pairs={{0,4},{2,6},{4,0},{6,2},{8,12},{10,14},{12,8},{14,10},{16,20},{18,... | collective-permute-start | bytes 1671176 | tf_op jit(solution)/shard_map/ppermute | solution.py:464
  4.6 16.6 %collective-permute-start = (bf16[4,544,128]{2,1,0:T(8,128)(2,1)}, bf16[4,544,128]{2,1,0:T(8,128)(2,1)}, u32[]{:S(2)}, u32[]{:S(2)}) collective-permute-start(bf16[4,544,128]{2,1,0:T(8,128)(2,1)} %get-tuple-element.25.refs_1_), channel_id=1, source_target_pairs={{0,2},{2,0},{4,6},{6,4},{8,10},{10,8},{12,14},{14,12},{16,18},{18,... | collective-permute-start | bytes 1671176 | tf_op jit(solution)/shard_map/ppermute | solution.py:464
  19.2 37.3 %collective-permute-start.3 = (bf16[4,544,128]{2,1,0:T(8,128)(2,1)}, bf16[4,544,128]{2,1,0:T(8,128)(2,1)}, u32[]{:S(2)}, u32[]{:S(2)}) collective-permute-start(bf16[4,544,128]{2,1,0:T(8,128)(2,1)} %collective-permute-done.1.refs_3_), channel_id=1, source_target_pairs={{0,8},{2,10},{4,12},{6,14},{8,16},{10,18},{12,20},{14,22},{16,24},... | collective-permute-start | bytes 1671176 | tf_op jit(solution)/shard_map/ppermute | solution.py:461
  20.5 36.1 %collective-permute-start.4 = (bf16[4,544,128]{2,1,0:T(8,128)(2,1)}, bf16[4,544,128]{2,1,0:T(8,128)(2,1)}, u32[]{:S(2)}, u32[]{:S(2)}) collective-permute-start(bf16[4,544,128]{2,1,0:T(8,128)(2,1)} %collective-permute-done.1.refs_3_), channel_id=1, source_target_pairs={{0,4},{2,6},{4,0},{6,2},{8,12},{10,14},{12,8},{14,10},{16,20},{18,... | collective-permute-start | bytes 1671176 | tf_op jit(solution)/shard_map/ppermute | solution.py:464
  56.6 17.5 %collective-permute-start.6 = (bf16[4,544,128]{2,1,0:T(8,128)(2,1)}, bf16[4,544,128]{2,1,0:T(8,128)(2,1)}, u32[]{:S(2)}, u32[]{:S(2)}) collective-permute-start(bf16[4,544,128]{2,1,0:T(8,128)(2,1)} %collective-permute-done.3.refs_1_), channel_id=1, source_target_pairs={{0,8},{2,10},{4,12},{6,14},{8,16},{10,18},{12,20},{14,22},{16,24},... | collective-permute-start | bytes 1671176 | tf_op jit(solution)/shard_map/ppermute | solution.py:461
  57.9 53.4 %collective-permute-start.7 = (bf16[4,544,128]{2,1,0:T(8,128)(2,1)}, bf16[4,544,128]{2,1,0:T(8,128)(2,1)}, u32[]{:S(2)}, u32[]{:S(2)}) collective-permute-start(bf16[4,544,128]{2,1,0:T(8,128)(2,1)} %collective-permute-done.3.refs_1_), channel_id=1, source_target_pairs={{0,4},{2,6},{4,0},{6,2},{8,12},{10,14},{12,8},{14,10},{16,20},{18,... | collective-permute-start | bytes 1671176 | tf_op jit(solution)/shard_map/ppermute | solution.py:464
  59.5 56.0 %collective-permute-start.13 = (bf16[4,544,128]{2,1,0:T(8,128)(2,1)}, bf16[4,544,128]{2,1,0:T(8,128)(2,1)}, u32[]{:S(2)}, u32[]{:S(2)}) collective-permute-start(bf16[4,544,128]{2,1,0:T(8,128)(2,1)} %collective-permute-done.1.refs_3_), channel_id=1, source_target_pairs={{0,2},{2,0},{4,6},{6,4},{8,10},{10,8},{12,14},{14,12},{16,18},{18,... | collective-permute-start | bytes 1671176 | tf_op jit(solution)/shard_map/ppermute | solution.py:464
  60.0 55.4 %collective-permute-start.12 = (bf16[4,544,128]{2,1,0:T(8,128)(2,1)}, bf16[4,544,128]{2,1,0:T(8,128)(2,1)}, u32[]{:S(2)}, u32[]{:S(2)}) collective-permute-start(bf16[4,544,128]{2,1,0:T(8,128)(2,1)} %collective-permute-done.2.refs_1_), channel_id=1, source_target_pairs={{0,2},{2,0},{4,6},{6,4},{8,10},{10,8},{12,14},{14,12},{16,18},{18,... | collective-permute-start | bytes 1671176 | tf_op jit(solution)/shard_map/ppermute | solution.py:464
  60.0 56.1 %collective-permute-start.14 = (bf16[4,544,128]{2,1,0:T(8,128)(2,1)}, bf16[4,544,128]{2,1,0:T(8,128)(2,1)}, u32[]{:S(2)}, u32[]{:S(2)}) collective-permute-start(bf16[4,544,128]{2,1,0:T(8,128)(2,1)} %collective-permute-done.4.refs_5_), channel_id=1, source_target_pairs={{0,2},{2,0},{4,6},{6,4},{8,10},{10,8},{12,14},{14,12},{16,18},{18,... | collective-permute-start | bytes 1671176 | tf_op jit(solution)/shard_map/ppermute | solution.py:464
  74.1 39.8 %collective-permute-start.15 = (f32[1,8,256]{2,1,0:T(8,128)}, f32[1,8,256]{2,1,0:T(8,128)}, u32[]{:S(2)}, u32[]{:S(2)}) collective-permute-start(f32[1,8,256]{2,1,0:T(8,128)} %loss.1.refs_12_), channel_id=1, source_target_pairs={{0,1},{1,0},{2,3},{3,2},{4,5},{5,4},{6,7},{7,6},{8,9},{9,8},{10,11... | collective-permute-start | bytes 24584 | tf_op jit(solution)/shard_map/ppermute | solution.py:484
  111.3 176.5 %collective-permute-start.5 = (bf16[4,544,128]{2,1,0:T(8,128)(2,1)}, bf16[4,544,128]{2,1,0:T(8,128)(2,1)}, u32[]{:S(2)}, u32[]{:S(2)}) collective-permute-start(bf16[4,544,128]{2,1,0:T(8,128)(2,1)} %collective-permute-done.3.refs_1_), channel_id=1, source_target_pairs={{0,2},{2,0},{4,6},{6,4},{8,10},{10,8},{12,14},{14,12},{16,18},{18,... | collective-permute-start | bytes 1671176 | tf_op jit(solution)/shard_map/ppermute | solution.py:464
  113.9 173.9 %collective-permute-start.10 = (bf16[4,544,128]{2,1,0:T(8,128)(2,1)}, bf16[4,544,128]{2,1,0:T(8,128)(2,1)}, u32[]{:S(2)}, u32[]{:S(2)}) collective-permute-start(bf16[4,544,128]{2,1,0:T(8,128)(2,1)} %collective-permute-done.6.refs_5_), channel_id=1, source_target_pairs={{0,4},{2,6},{4,0},{6,2},{8,12},{10,14},{12,8},{14,10},{16,20},{18,... | collective-permute-start | bytes 1671176 | tf_op jit(solution)/shard_map/ppermute | solution.py:464
  115.4 172.4 %collective-permute-start.11 = (bf16[4,544,128]{2,1,0:T(8,128)(2,1)}, bf16[4,544,128]{2,1,0:T(8,128)(2,1)}, u32[]{:S(2)}, u32[]{:S(2)}) collective-permute-start(bf16[4,544,128]{2,1,0:T(8,128)(2,1)} %collective-permute-done.6.refs_5_), channel_id=1, source_target_pairs={{0,6},{2,4},{4,2},{6,0},{8,14},{10,12},{12,10},{14,8},{16,22},{18,... | collective-permute-start | bytes 1671176 | tf_op jit(solution)/shard_map/ppermute | solution.py:464
  115.4 172.4 %collective-permute-start.9 = (bf16[4,544,128]{2,1,0:T(8,128)(2,1)}, bf16[4,544,128]{2,1,0:T(8,128)(2,1)}, u32[]{:S(2)}, u32[]{:S(2)}) collective-permute-start(bf16[4,544,128]{2,1,0:T(8,128)(2,1)} %collective-permute-done.6.refs_5_), channel_id=1, source_target_pairs={{0,2},{2,0},{4,6},{6,4},{8,10},{10,8},{12,14},{14,12},{16,18},{18,... | collective-permute-start | bytes 1671176 | tf_op jit(solution)/shard_map/ppermute | solution.py:464
  116.1 171.8 %collective-permute-start.8 = (bf16[4,544,128]{2,1,0:T(8,128)(2,1)}, bf16[4,544,128]{2,1,0:T(8,128)(2,1)}, u32[]{:S(2)}, u32[]{:S(2)}) collective-permute-start(bf16[4,544,128]{2,1,0:T(8,128)(2,1)} %collective-permute-done.7.refs_3_), channel_id=1, source_target_pairs={{0,2},{2,0},{4,6},{6,4},{8,10},{10,8},{12,14},{14,12},{16,18},{18,... | collective-permute-start | bytes 1671176 | tf_op jit(solution)/shard_map/ppermute | solution.py:464

commit v4 on v3

--- a/solution.py
+++ b/solution.py
@@ -259,8 +259,9 @@
         for begin in range(pairs % 2, pairs, 2):
             a, b = begin, begin + 1
             plain = begin < 2
+            trio = jnp.logical_and(pairs == 3, full[0] & full[1] & full[pairs - 1])
             if plain:
-                both = full[a] & full[b]
+                both = full[a] & full[b] & jnp.logical_not(trio)
             else:
                 both = some[a] & some[b] & jnp.logical_not(half[a] | half[b])
             together[a] = together[b] = both
@@ -270,9 +271,17 @@
             def _():
                 visit([a, b], not plain, opens)
 
+            if pairs == 3:
+
+                @pl.when(trio)
+                def _():
+                    visit([0, 1, 2], False, True)
+
+                together = {pair: both | trio if pair else trio for pair in range(3)}
+
             if opens:
 
-                @pl.when(jnp.logical_not(both))
+                @pl.when(jnp.logical_not(both | trio))
                 def _():
                     for g in range(group):
                         acc_out[0, g] = acc_in[0, g]
@@ -406,25 +415,35 @@
     def _(b):
         here = pl.ds(pl.multiple_of(b * SUB, SUB), SUB)
         peak = x_ref[here, 0:step]
-        for c in range(1, width // step):
-            peak = jnp.maximum(peak, x_ref[here, c * step : (c + 1) * step])
+        total = jnp.zeros((SUB, wide), F32)
+        for c in range(width // step):
+            x = x_ref[here, c * step : (c + 1) * step]
+            peak = jnp.maximum(peak, x)
+            for h in range(step // wide):
+                total = total + jnp.exp2(x[:, h * wide : (h + 1) * wide].astype(F32) * LOG2E)
         peak = jnp.max(peak.astype(F32), axis=1, keepdims=True)
-        total = jnp.zeros((SUB, wide), F32)
-        for c in range(width // wide):
-            x = x_ref[here, c * wide : (c + 1) * wide].astype(F32)
-            total = total + jnp.exp2((x - peak) * LOG2E)
         total = jnp.sum(total, axis=1, keepdims=True)
-        hit = jnp.zeros((SUB, HD), F32)
+        near = jnp.zeros((SUB, HD), F32)
+        spot = jnp.full((SUB, HD), -1, jnp.int32)
         for r in range(SUB):
             t = tgt_ref[first + b * SUB + r] - start_col
             inside = (t >= 0) & (t < width)
             lane = jnp.where(inside, t, 0)
             start = pl.multiple_of((lane // HD) * HD, HD)
-            x = x_ref[here, pl.ds(start, HD)].astype(F32)
-            hit = jnp.where((row_at == r) & (lane_at == lane - start) & inside, x, hit)
-        hit = jnp.sum(hit, axis=1, keepdims=True)
+            near = jnp.where(row_at == r, x_ref[here, pl.ds(start, HD)].astype(F32), near)
+            spot = jnp.where(row_at == r, jnp.where(inside, lane - start, -1), spot)
+        hit = jnp.sum(jnp.where(lane_at == spot, near, 0.0), axis=1, keepdims=True)
         there = pl.ds(pl.multiple_of(first + b * SUB, SUB), SUB)
-        all_ref[there, :] = jnp.where(lane_at == 0, peak, jnp.where(lane_at == 1, total, hit))
+        all_ref[there, :] = jnp.where(lane_at == 1, total, jnp.where(lane_at == 2, hit, 0.0))
+
+        @pl.when(jnp.max(jnp.abs(peak)) * LOG2E > LIMIT)
+        def _():
+            exact = jnp.zeros((SUB, wide), F32)
+            for c in range(width // wide):
+                x = x_ref[here, c * wide : (c + 1) * wide].astype(F32)
+                exact = exact + jnp.exp2((x - peak) * LOG2E)
+            exact = jnp.sum(exact, axis=1, keepdims=True)
+            all_ref[there, :] = jnp.where(lane_at == 0, peak, jnp.where(lane_at == 1, exact, hit))
 
     @pl.when(i == pl.num_programs(0) - 1)
     def _():

time: 464 us -> 464 us (level)
  transfers between devices with their start and end apart: 16 -> 16, of which waited for: 2 -> 1; matrix products, arithmetic and copies ran while one was open for 0% -> 0% of each run, Pallas kernels for 55% -> 55%
where the time goes in v4:
time: 464 us; the launch traced here: 463 us
  Pallas kernels  433 us (93%)
  starting transfers between devices  16.3 us (4%)
  waiting for transfers between devices  12.9 us (3%)
    pallas_call x4, Pallas kernels, stage(): pl.pallas_call(functools.partial(stage_kernel, group, rows, steps, source...  415 us
    pallas_call x1, Pallas kernels, loss_parts(): pl.pallas_call(functools.partial(loss_kernel, block, width), grid_spec=pl...  16.7 us
    ppermute x3, waiting for transfers between devices, up(): return lax.ppermute(x, 'seq', [(i, i + 4) for i in range(shards - 4)])  12.8 us
    ppermute x12, starting transfers between devices, swap(): return lax.ppermute(x, 'seq', [(i, i ^ bit) for i in range(shards)])  11 us
  transfers between devices with their start and end apart: 16, of which 1 were waited for; matrix products, arithmetic and copies ran while one was open for 0% of the time, Pallas kernels for 55%

profile of v4, /device:TPU:26, one launch (start us, length us, event | category | flops | bytes accessed | tf_op | source)
XLA Modules:
  0.0 463.3 jit_solution(2183789463888937452)
XLA Ops:
  0.6 2.0 pack.1
  2.7 1.3 collective-permute-start.1
  4.0 0.6 collective-permute-start.2
  4.6 0.0 collective-permute-start
  4.6 16.7 %loss.1.refs_12_ = f32[1,8,256]{2,1,0:T(8,128)} custom-call(s32[256]{0:T(256)} %tgt_ref.1, bf16[256,32768]{1,0:T(8,128)(2,1)} %x_ref.1), custom_call_target="tpu_custom_call" | custom-call | flops 33554432 | bytes 16777216 | tf_op jit(solution)/shard_map/loss/pallas_call | solution.py:456
  21.2 0.0 collective-permute-done.1.refs_3_
  21.2 0.0 collective-permute-done.2.refs_1_
  21.2 1.3 collective-permute-start.3
  22.5 1.6 collective-permute-start.4
  24.1 0.0 collective-permute-done.refs_2_
  24.1 35.5 %stage_first.2 = (f32[12,8,136,256]{3,2,1,0:T(8,128)}, f32[12,2,8,256]{3,2,1,0:T(8,128)}, bf16[12,8,256,128]{3,2,1,0:T(8,128)(2,1)}) custom-call(s32[256]{0:T(256)} %doc_ref.7, bf16[3,256,4096]{2,1,0:T(8,128)(2,1)} %refs_0_.3, bf16[4,544,128]{2,1,0:T(8,128)(2,1)} %get-tuple-element.25.refs_1_, bf16[4,544,128]{2,1,0:T(8,128)(2,1)} %collective-permute-done.refs_2_, ...), custom_call_target="tpu_custom_call" | custom-call | flops 3221225472 | bytes 12582912 | tf_op jit(solution)/shard_map/stage_first/pallas_call | solution.py:384
  59.5 0.0 collective-permute-done.3.refs_1_
  59.5 0.0 collective-permute-done.4.refs_5_
  59.5 1.3 collective-permute-start.6
  60.8 0.6 collective-permute-start.7
  61.4 2.1 collective-permute-start.13
  63.5 0.0 collective-permute-start.12
  63.5 0.5 collective-permute-start.14
  64.0 12.8 %collective-permute-done.6.refs_5_ = bf16[4,544,128]{2,1,0:T(8,128)(2,1)} collective-permute-done((bf16[4,544,128]{2,1,0:T(8,128)(2,1)}, bf16[4,544,128]{2,1,0:T(8,128)(2,1)}, u32[]{:S(2)}, u32[]{:S(2)}) %collective-permute-start.6) | collective-permute-done | bytes 557088 | tf_op jit(solution)/shard_map/ppermute | solution.py:480
  76.8 1.5 collective-permute-start.15
  78.4 35.5 %stage_first.3 = (f32[12,8,136,256]{3,2,1,0:T(8,128)}, f32[12,2,8,256]{3,2,1,0:T(8,128)}, bf16[12,8,256,128]{3,2,1,0:T(8,128)(2,1)}) custom-call(s32[256]{0:T(256)} %doc_ref.7, bf16[3,256,4096]{2,1,0:T(8,128)(2,1)} %refs_0_.3, bf16[4,544,128]{2,1,0:T(8,128)(2,1)} %get-tuple-element.25.refs_1_, ...), custom_call_target="tpu_custom_call", output_to_operand_aliasing={{0}: (6, {}), {1}: (7, {}), {2}: (8, {})} | custom-call | flops 3221225472 | bytes 12582912 | tf_op jit(solution)/shard_map/stage_first/pallas_call | solution.py:384
  113.9 0.0 collective-permute-done.7.refs_3_
  113.9 3.4 collective-permute-start.5
  117.3 0.0 collective-permute-done.15.refs_13_
  117.3 0.5 collective-permute-start.10
  117.8 0.0 collective-permute-done.13.refs_4_
  117.8 0.9 collective-permute-start.11
  118.7 0.0 collective-permute-done.12.refs_2_
  118.7 0.7 collective-permute-start.9
  119.5 0.0 collective-permute-done.14.refs_6_
  119.5 0.1 collective-permute-start.8
  119.5 168.9 %stage_mid.1 = (f32[12,8,136,256]{3,2,1,0:T(8,128)}, f32[12,2,8,256]{3,2,1,0:T(8,128)}) custom-call(s32[256]{0:T(256)} %doc_ref.7, bf16[12,8,256,128]{3,2,1,0:T(8,128)(2,1)} %get-tuple-element.32.refs_0_, bf16[4,544,128]{2,1,0:T(8,128)(2,1)} %collective-permute-done.2.refs_1_, ...), custom_call_target="tpu_custom_call", output_to_operand_aliasing={{0}: (9, {}), {1}: (10, {})} | custom-call | flops 19327352832 | bytes 12582912 | tf_op jit(solution)/shard_map/stage_mid/pallas_call | solution.py:384
  288.4 0.0 collective-permute-done.5.refs_2_
  288.4 0.0 collective-permute-done.10.refs_7_
  288.4 0.0 collective-permute-done.11.refs_8_
  288.4 0.0 collective-permute-done.8.refs_4_
  288.4 0.0 collective-permute-done.9.refs_6_
  288.4 174.7 %stage_last.1 = (bf16[3,256,4096]{2,1,0:T(8,128)(2,1)}, f32[3,32,256]{2,1,0:T(8,128)}, f32[1,256]{1,0:T(1,128)}) custom-call(s32[256]{0:T(256)} %doc_ref.7, bf16[12,8,256,128]{3,2,1,0:T(8,128)(2,1)} %get-tuple-element.32.refs_0_, bf16[4,544,128]{2,1,0:T(8,128)(2,1)} %collective-permute-done.3.refs_1_, bf16[4,544,128]{2,1,0:T(8,128)(2,1)} %collective-permute-done.5.refs_2_, ...), custom_call_target="tpu_custom_call" | custom-call | flops 25769803776 | bytes 12582912 | tf_op jit(solution)/shard_map/stage_last/pallas_call | solution.py:384
Async XLA Ops:
  2.7 18.6 %collective-permute-start.1 = (bf16[4,544,128]{2,1,0:T(8,128)(2,1)}, bf16[4,544,128]{2,1,0:T(8,128)(2,1)}, u32[]{:S(2)}, u32[]{:S(2)}) collective-permute-start(bf16[4,544,128]{2,1,0:T(8,128)(2,1)} %get-tuple-element.25.refs_1_), channel_id=1, source_target_pairs={{0,8},{2,10},{4,12},{6,14},{8,16},{10,18},{12,20},{14,22},{16,24},... | collective-permute-start | bytes 1671176 | tf_op jit(solution)/shard_map/ppermute | solution.py:480
  4.0 17.3 %collective-permute-start.2 = (bf16[4,544,128]{2,1,0:T(8,128)(2,1)}, bf16[4,544,128]{2,1,0:T(8,128)(2,1)}, u32[]{:S(2)}, u32[]{:S(2)}) collective-permute-start(bf16[4,544,128]{2,1,0:T(8,128)(2,1)} %get-tuple-element.25.refs_1_), channel_id=1, source_target_pairs={{0,4},{2,6},{4,0},{6,2},{8,12},{10,14},{12,8},{14,10},{16,20},{18,... | collective-permute-start | bytes 1671176 | tf_op jit(solution)/shard_map/ppermute | solution.py:483
  4.6 19.5 %collective-permute-start = (bf16[4,544,128]{2,1,0:T(8,128)(2,1)}, bf16[4,544,128]{2,1,0:T(8,128)(2,1)}, u32[]{:S(2)}, u32[]{:S(2)}) collective-permute-start(bf16[4,544,128]{2,1,0:T(8,128)(2,1)} %get-tuple-element.25.refs_1_), channel_id=1, source_target_pairs={{0,2},{2,0},{4,6},{6,4},{8,10},{10,8},{12,14},{14,12},{16,18},{18,... | collective-permute-start | bytes 1671176 | tf_op jit(solution)/shard_map/ppermute | solution.py:483
  21.2 38.3 %collective-permute-start.3 = (bf16[4,544,128]{2,1,0:T(8,128)(2,1)}, bf16[4,544,128]{2,1,0:T(8,128)(2,1)}, u32[]{:S(2)}, u32[]{:S(2)}) collective-permute-start(bf16[4,544,128]{2,1,0:T(8,128)(2,1)} %collective-permute-done.1.refs_3_), channel_id=1, source_target_pairs={{0,8},{2,10},{4,12},{6,14},{8,16},{10,18},{12,20},{14,22},{16,24},... | collective-permute-start | bytes 1671176 | tf_op jit(solution)/shard_map/ppermute | solution.py:480
  22.5 37.0 %collective-permute-start.4 = (bf16[4,544,128]{2,1,0:T(8,128)(2,1)}, bf16[4,544,128]{2,1,0:T(8,128)(2,1)}, u32[]{:S(2)}, u32[]{:S(2)}) collective-permute-start(bf16[4,544,128]{2,1,0:T(8,128)(2,1)} %collective-permute-done.1.refs_3_), channel_id=1, source_target_pairs={{0,4},{2,6},{4,0},{6,2},{8,12},{10,14},{12,8},{14,10},{16,20},{18,... | collective-permute-start | bytes 1671176 | tf_op jit(solution)/shard_map/ppermute | solution.py:483
  59.5 17.3 %collective-permute-start.6 = (bf16[4,544,128]{2,1,0:T(8,128)(2,1)}, bf16[4,544,128]{2,1,0:T(8,128)(2,1)}, u32[]{:S(2)}, u32[]{:S(2)}) collective-permute-start(bf16[4,544,128]{2,1,0:T(8,128)(2,1)} %collective-permute-done.3.refs_1_), channel_id=1, source_target_pairs={{0,8},{2,10},{4,12},{6,14},{8,16},{10,18},{12,20},{14,22},{16,24},... | collective-permute-start | bytes 1671176 | tf_op jit(solution)/shard_map/ppermute | solution.py:480
  60.8 53.0 %collective-permute-start.7 = (bf16[4,544,128]{2,1,0:T(8,128)(2,1)}, bf16[4,544,128]{2,1,0:T(8,128)(2,1)}, u32[]{:S(2)}, u32[]{:S(2)}) collective-permute-start(bf16[4,544,128]{2,1,0:T(8,128)(2,1)} %collective-permute-done.3.refs_1_), channel_id=1, source_target_pairs={{0,4},{2,6},{4,0},{6,2},{8,12},{10,14},{12,8},{14,10},{16,20},{18,... | collective-permute-start | bytes 1671176 | tf_op jit(solution)/shard_map/ppermute | solution.py:483
  61.4 56.4 %collective-permute-start.13 = (bf16[4,544,128]{2,1,0:T(8,128)(2,1)}, bf16[4,544,128]{2,1,0:T(8,128)(2,1)}, u32[]{:S(2)}, u32[]{:S(2)}) collective-permute-start(bf16[4,544,128]{2,1,0:T(8,128)(2,1)} %collective-permute-done.1.refs_3_), channel_id=1, source_target_pairs={{0,2},{2,0},{4,6},{6,4},{8,10},{10,8},{12,14},{14,12},{16,18},{18,... | collective-permute-start | bytes 1671176 | tf_op jit(solution)/shard_map/ppermute | solution.py:483
  63.5 55.2 %collective-permute-start.12 = (bf16[4,544,128]{2,1,0:T(8,128)(2,1)}, bf16[4,544,128]{2,1,0:T(8,128)(2,1)}, u32[]{:S(2)}, u32[]{:S(2)}) collective-permute-start(bf16[4,544,128]{2,1,0:T(8,128)(2,1)} %collective-permute-done.2.refs_1_), channel_id=1, source_target_pairs={{0,2},{2,0},{4,6},{6,4},{8,10},{10,8},{12,14},{14,12},{16,18},{18,... | collective-permute-start | bytes 1671176 | tf_op jit(solution)/shard_map/ppermute | solution.py:483
  63.5 55.9 %collective-permute-start.14 = (bf16[4,544,128]{2,1,0:T(8,128)(2,1)}, bf16[4,544,128]{2,1,0:T(8,128)(2,1)}, u32[]{:S(2)}, u32[]{:S(2)}) collective-permute-start(bf16[4,544,128]{2,1,0:T(8,128)(2,1)} %collective-permute-done.4.refs_5_), channel_id=1, source_target_pairs={{0,2},{2,0},{4,6},{6,4},{8,10},{10,8},{12,14},{14,12},{16,18},{18,... | collective-permute-start | bytes 1671176 | tf_op jit(solution)/shard_map/ppermute | solution.py:483
  76.8 40.5 %collective-permute-start.15 = (f32[1,8,256]{2,1,0:T(8,128)}, f32[1,8,256]{2,1,0:T(8,128)}, u32[]{:S(2)}, u32[]{:S(2)}) collective-permute-start(f32[1,8,256]{2,1,0:T(8,128)} %loss.1.refs_12_), channel_id=1, source_target_pairs={{0,1},{1,0},{2,3},{3,2},{4,5},{5,4},{6,7},{7,6},{8,9},{9,8},{10,11... | collective-permute-start | bytes 24584 | tf_op jit(solution)/shard_map/ppermute | solution.py:503
  113.9 174.5 %collective-permute-start.5 = (bf16[4,544,128]{2,1,0:T(8,128)(2,1)}, bf16[4,544,128]{2,1,0:T(8,128)(2,1)}, u32[]{:S(2)}, u32[]{:S(2)}) collective-permute-start(bf16[4,544,128]{2,1,0:T(8,128)(2,1)} %collective-permute-done.3.refs_1_), channel_id=1, source_target_pairs={{0,2},{2,0},{4,6},{6,4},{8,10},{10,8},{12,14},{14,12},{16,18},{18,... | collective-permute-start | bytes 1671176 | tf_op jit(solution)/shard_map/ppermute | solution.py:483
  117.3 171.1 %collective-permute-start.10 = (bf16[4,544,128]{2,1,0:T(8,128)(2,1)}, bf16[4,544,128]{2,1,0:T(8,128)(2,1)}, u32[]{:S(2)}, u32[]{:S(2)}) collective-permute-start(bf16[4,544,128]{2,1,0:T(8,128)(2,1)} %collective-permute-done.6.refs_5_), channel_id=1, source_target_pairs={{0,4},{2,6},{4,0},{6,2},{8,12},{10,14},{12,8},{14,10},{16,20},{18,... | collective-permute-start | bytes 1671176 | tf_op jit(solution)/shard_map/ppermute | solution.py:483
  117.8 170.6 %collective-permute-start.11 = (bf16[4,544,128]{2,1,0:T(8,128)(2,1)}, bf16[4,544,128]{2,1,0:T(8,128)(2,1)}, u32[]{:S(2)}, u32[]{:S(2)}) collective-permute-start(bf16[4,544,128]{2,1,0:T(8,128)(2,1)} %collective-permute-done.6.refs_5_), channel_id=1, source_target_pairs={{0,6},{2,4},{4,2},{6,0},{8,14},{10,12},{12,10},{14,8},{16,22},{18,... | collective-permute-start | bytes 1671176 | tf_op jit(solution)/shard_map/ppermute | solution.py:483
  118.7 169.7 %collective-permute-start.9 = (bf16[4,544,128]{2,1,0:T(8,128)(2,1)}, bf16[4,544,128]{2,1,0:T(8,128)(2,1)}, u32[]{:S(2)}, u32[]{:S(2)}) collective-permute-start(bf16[4,544,128]{2,1,0:T(8,128)(2,1)} %collective-permute-done.6.refs_5_), channel_id=1, source_target_pairs={{0,2},{2,0},{4,6},{6,4},{8,10},{10,8},{12,14},{14,12},{16,18},{18,... | collective-permute-start | bytes 1671176 | tf_op jit(solution)/shard_map/ppermute | solution.py:483
  119.5 169.0 %collective-permute-start.8 = (bf16[4,544,128]{2,1,0:T(8,128)(2,1)}, bf16[4,544,128]{2,1,0:T(8,128)(2,1)}, u32[]{:S(2)}, u32[]{:S(2)}) collective-permute-start(bf16[4,544,128]{2,1,0:T(8,128)(2,1)} %collective-permute-done.7.refs_3_), channel_id=1, source_target_pairs={{0,2},{2,0},{4,6},{6,4},{8,10},{10,8},{12,14},{14,12},{16,18},{18,... | collective-permute-start | bytes 1671176 | tf_op jit(solution)/shard_map/ppermute | solution.py:483

commit v5 on v4

--- a/solution.py
+++ b/solution.py
@@ -162,8 +162,11 @@
             if n >= late:
                 g, pair, p = waiting.pop(0)
                 more = jnp.dot(vts[pair], p, preferred_element_type=F32)[0:KEEP]
-                old = acc_in if fresh and pair == chosen[0] else acc_out
-                acc_out[0, g] = old[0, g] + (more if first else jnp.where(lead, more, 0.0))
+                if first:
+                    acc_out[0, g] = more
+                else:
+                    old = acc_in if fresh and pair == chosen[0] else acc_out
+                    acc_out[0, g] = old[0, g] + jnp.where(lead, more, 0.0)
 
     def revisit(pair):
         ok = usable(pair)
@@ -212,13 +215,10 @@
         top_out[0, 0] = jnp.zeros((group, rows), F32)
         top_out[0, 1] = functools.reduce(jnp.maximum, [own_s[i] for i in range(1, steps)])
 
-        def start():
+        def add_drafts():
             weights = [jnp.exp2((own_s[i] - top_out[0, 0]) * c2) for i in range(1, steps)]
             for g in range(group):
-                acc_out[0, g, 0:HD] = jnp.zeros((HD, rows), F32)
-                acc_out[0, g, HD:KEEP] = jnp.broadcast_to(
-                    functools.reduce(jnp.add, weights)[g : g + 1, :], (KEEP - HD, rows)
-                )
+                acc_out[0, g, HD:KEEP] = acc_out[0, g, HD:KEEP] + functools.reduce(jnp.add, weights)[g : g + 1, :]
             for i in range(1, steps):
 
                 @pl.when(step >= i)
@@ -228,23 +228,23 @@
                         w = weights[i - 1][g : g + 1, :].astype(BF16).astype(F32)
                         acc_out[0, g, 0:HD] = acc_out[0, g, 0:HD] + own_val * w
 
-        start()
-
         @pl.when(count_ref[1] < rows)
         def _():
-            visit([0], True, False)
+            visit([0], True, True)
 
         @pl.when(count_ref[1] >= rows)
         def _():
-            visit([0], True, False, 1)
-
+            visit([0], True, True, 1)
+
+        add_drafts()
         spread = jnp.max(jnp.abs(top_out[0, 1])) * c2
 
         @pl.when(spread > LIMIT)
         def _():
             top_out[0, 0] = top_out[0, 1]
-            start()
+            acc_out[...] = jnp.zeros_like(acc_out)
             revisit(0)
+            add_drafts()
 
     else:
         top_out[...] = top_in[...]
@@ -298,7 +298,7 @@
                 visit([pair], True, False, 1)
 
         past = top_in[0, 0]
-        spread = jnp.maximum(jnp.max(top_out[0, 1]) * c2 - LIMIT, jnp.max(jnp.abs(past)))
+        spread = jnp.max(jnp.maximum(top_out[0, 1] * c2 - LIMIT, jnp.abs(past)))
 
         @pl.when(spread > 0.0)
         def _():

time: 464 us -> 464 us (level)
  no operation moved by 1% of the time
where the time goes in v5:
time: 464 us; the launch traced here: 463 us
  Pallas kernels  433 us (93%)
  starting transfers between devices  16.3 us (4%)
  waiting for transfers between devices  12.9 us (3%)
    pallas_call x4, Pallas kernels, stage(): pl.pallas_call(functools.partial(stage_kernel, group, rows, steps, source...  414 us
    pallas_call x1, Pallas kernels, loss_parts(): pl.pallas_call(functools.partial(loss_kernel, block, width), grid_spec=pl...  16.7 us
    ppermute x3, waiting for transfers between devices, up(): return lax.ppermute(x, 'seq', [(i, i + 4) for i in range(shards - 4)])  12.9 us
    ppermute x12, starting transfers between devices, swap(): return lax.ppermute(x, 'seq', [(i, i ^ bit) for i in range(shards)])  10.9 us
  transfers between devices with their start and end apart: 16, of which 1 were waited for; matrix products, arithmetic and copies ran while one was open for 0% of the time, Pallas kernels for 55%

profile of v5, /device:TPU:26, one launch (start us, length us, event | category | flops | bytes accessed | tf_op | source)
XLA Modules:
  0.0 462.8 jit_solution(15420844352668585063)
XLA Ops:
  0.6 2.0 pack.1
  2.7 1.3 collective-permute-start.1
  4.0 0.6 collective-permute-start.2
  4.6 0.0 collective-permute-start
  4.6 16.7 %loss.1.refs_12_ = f32[1,8,256]{2,1,0:T(8,128)} custom-call(s32[256]{0:T(256)} %tgt_ref.1, bf16[256,32768]{1,0:T(8,128)(2,1)} %x_ref.1), custom_call_target="tpu_custom_call" | custom-call | flops 33554432 | bytes 16777216 | tf_op jit(solution)/shard_map/loss/pallas_call | solution.py:456
  21.2 0.0 collective-permute-done.1.refs_3_
  21.2 0.0 collective-permute-done.2.refs_1_
  21.2 1.3 collective-permute-start.3
  22.5 1.6 collective-permute-start.4
  24.1 0.0 collective-permute-done.refs_2_
  24.1 35.2 %stage_first.2 = (f32[12,8,136,256]{3,2,1,0:T(8,128)}, f32[12,2,8,256]{3,2,1,0:T(8,128)}, bf16[12,8,256,128]{3,2,1,0:T(8,128)(2,1)}) custom-call(s32[256]{0:T(256)} %doc_ref.7, bf16[3,256,4096]{2,1,0:T(8,128)(2,1)} %refs_0_.3, bf16[4,544,128]{2,1,0:T(8,128)(2,1)} %get-tuple-element.25.refs_1_, bf16[4,544,128]{2,1,0:T(8,128)(2,1)} %collective-permute-done.refs_2_, ...), custom_call_target="tpu_custom_call" | custom-call | flops 3221225472 | bytes 12582912 | tf_op jit(solution)/shard_map/stage_first/pallas_call | solution.py:384
  59.2 0.0 collective-permute-done.3.refs_1_
  59.2 0.0 collective-permute-done.4.refs_5_
  59.2 1.3 collective-permute-start.6
  60.5 0.6 collective-permute-start.7
  61.1 2.0 collective-permute-start.13
  63.2 0.0 collective-permute-start.12
  63.2 0.5 collective-permute-start.14
  63.7 12.8 %collective-permute-done.6.refs_5_ = bf16[4,544,128]{2,1,0:T(8,128)(2,1)} collective-permute-done((bf16[4,544,128]{2,1,0:T(8,128)(2,1)}, bf16[4,544,128]{2,1,0:T(8,128)(2,1)}, u32[]{:S(2)}, u32[]{:S(2)}) %collective-permute-start.6) | collective-permute-done | bytes 557088 | tf_op jit(solution)/shard_map/ppermute | solution.py:480
  76.6 1.5 collective-permute-start.15
  78.1 35.2 %stage_first.3 = (f32[12,8,136,256]{3,2,1,0:T(8,128)}, f32[12,2,8,256]{3,2,1,0:T(8,128)}, bf16[12,8,256,128]{3,2,1,0:T(8,128)(2,1)}) custom-call(s32[256]{0:T(256)} %doc_ref.7, bf16[3,256,4096]{2,1,0:T(8,128)(2,1)} %refs_0_.3, bf16[4,544,128]{2,1,0:T(8,128)(2,1)} %get-tuple-element.25.refs_1_, ...), custom_call_target="tpu_custom_call", output_to_operand_aliasing={{0}: (6, {}), {1}: (7, {}), {2}: (8, {})} | custom-call | flops 3221225472 | bytes 12582912 | tf_op jit(solution)/shard_map/stage_first/pallas_call | solution.py:384
  113.3 0.0 collective-permute-done.7.refs_3_
  113.3 3.4 collective-permute-start.5
  116.7 0.0 collective-permute-done.15.refs_13_
  116.7 0.5 collective-permute-start.10
  117.2 0.0 collective-permute-done.13.refs_4_
  117.2 0.9 collective-permute-start.11
  118.1 0.0 collective-permute-done.12.refs_2_
  118.1 0.7 collective-permute-start.9
  118.8 0.0 collective-permute-done.14.refs_6_
  118.8 0.1 collective-permute-start.8
  118.9 169.0 %stage_mid.1 = (f32[12,8,136,256]{3,2,1,0:T(8,128)}, f32[12,2,8,256]{3,2,1,0:T(8,128)}) custom-call(s32[256]{0:T(256)} %doc_ref.7, bf16[12,8,256,128]{3,2,1,0:T(8,128)(2,1)} %get-tuple-element.32.refs_0_, bf16[4,544,128]{2,1,0:T(8,128)(2,1)} %collective-permute-done.2.refs_1_, ...), custom_call_target="tpu_custom_call", output_to_operand_aliasing={{0}: (9, {}), {1}: (10, {})} | custom-call | flops 19327352832 | bytes 12582912 | tf_op jit(solution)/shard_map/stage_mid/pallas_call | solution.py:384
  287.9 0.0 collective-permute-done.5.refs_2_
  287.9 0.0 collective-permute-done.10.refs_7_
  287.9 0.0 collective-permute-done.11.refs_8_
  287.9 0.0 collective-permute-done.8.refs_4_
  287.9 0.0 collective-permute-done.9.refs_6_
  287.9 174.7 %stage_last.1 = (bf16[3,256,4096]{2,1,0:T(8,128)(2,1)}, f32[3,32,256]{2,1,0:T(8,128)}, f32[1,256]{1,0:T(1,128)}) custom-call(s32[256]{0:T(256)} %doc_ref.7, bf16[12,8,256,128]{3,2,1,0:T(8,128)(2,1)} %get-tuple-element.32.refs_0_, bf16[4,544,128]{2,1,0:T(8,128)(2,1)} %collective-permute-done.3.refs_1_, bf16[4,544,128]{2,1,0:T(8,128)(2,1)} %collective-permute-done.5.refs_2_, ...), custom_call_target="tpu_custom_call" | custom-call | flops 25769803776 | bytes 12582912 | tf_op jit(solution)/shard_map/stage_last/pallas_call | solution.py:384
Async XLA Ops:
  2.7 18.6 %collective-permute-start.1 = (bf16[4,544,128]{2,1,0:T(8,128)(2,1)}, bf16[4,544,128]{2,1,0:T(8,128)(2,1)}, u32[]{:S(2)}, u32[]{:S(2)}) collective-permute-start(bf16[4,544,128]{2,1,0:T(8,128)(2,1)} %get-tuple-element.25.refs_1_), channel_id=1, source_target_pairs={{0,8},{2,10},{4,12},{6,14},{8,16},{10,18},{12,20},{14,22},{16,24},... | collective-permute-start | bytes 1671176 | tf_op jit(solution)/shard_map/ppermute | solution.py:480
  4.0 17.3 %collective-permute-start.2 = (bf16[4,544,128]{2,1,0:T(8,128)(2,1)}, bf16[4,544,128]{2,1,0:T(8,128)(2,1)}, u32[]{:S(2)}, u32[]{:S(2)}) collective-permute-start(bf16[4,544,128]{2,1,0:T(8,128)(2,1)} %get-tuple-element.25.refs_1_), channel_id=1, source_target_pairs={{0,4},{2,6},{4,0},{6,2},{8,12},{10,14},{12,8},{14,10},{16,20},{18,... | collective-permute-start | bytes 1671176 | tf_op jit(solution)/shard_map/ppermute | solution.py:483
  4.6 19.5 %collective-permute-start = (bf16[4,544,128]{2,1,0:T(8,128)(2,1)}, bf16[4,544,128]{2,1,0:T(8,128)(2,1)}, u32[]{:S(2)}, u32[]{:S(2)}) collective-permute-start(bf16[4,544,128]{2,1,0:T(8,128)(2,1)} %get-tuple-element.25.refs_1_), channel_id=1, source_target_pairs={{0,2},{2,0},{4,6},{6,4},{8,10},{10,8},{12,14},{14,12},{16,18},{18,... | collective-permute-start | bytes 1671176 | tf_op jit(solution)/shard_map/ppermute | solution.py:483
  21.2 38.0 %collective-permute-start.3 = (bf16[4,544,128]{2,1,0:T(8,128)(2,1)}, bf16[4,544,128]{2,1,0:T(8,128)(2,1)}, u32[]{:S(2)}, u32[]{:S(2)}) collective-permute-start(bf16[4,544,128]{2,1,0:T(8,128)(2,1)} %collective-permute-done.1.refs_3_), channel_id=1, source_target_pairs={{0,8},{2,10},{4,12},{6,14},{8,16},{10,18},{12,20},{14,22},{16,24},... | collective-permute-start | bytes 1671176 | tf_op jit(solution)/shard_map/ppermute | solution.py:480
  22.5 36.7 %collective-permute-start.4 = (bf16[4,544,128]{2,1,0:T(8,128)(2,1)}, bf16[4,544,128]{2,1,0:T(8,128)(2,1)}, u32[]{:S(2)}, u32[]{:S(2)}) collective-permute-start(bf16[4,544,128]{2,1,0:T(8,128)(2,1)} %collective-permute-done.1.refs_3_), channel_id=1, source_target_pairs={{0,4},{2,6},{4,0},{6,2},{8,12},{10,14},{12,8},{14,10},{16,20},{18,... | collective-permute-start | bytes 1671176 | tf_op jit(solution)/shard_map/ppermute | solution.py:483
  59.2 17.3 %collective-permute-start.6 = (bf16[4,544,128]{2,1,0:T(8,128)(2,1)}, bf16[4,544,128]{2,1,0:T(8,128)(2,1)}, u32[]{:S(2)}, u32[]{:S(2)}) collective-permute-start(bf16[4,544,128]{2,1,0:T(8,128)(2,1)} %collective-permute-done.3.refs_1_), channel_id=1, source_target_pairs={{0,8},{2,10},{4,12},{6,14},{8,16},{10,18},{12,20},{14,22},{16,24},... | collective-permute-start | bytes 1671176 | tf_op jit(solution)/shard_map/ppermute | solution.py:480
  60.5 52.7 %collective-permute-start.7 = (bf16[4,544,128]{2,1,0:T(8,128)(2,1)}, bf16[4,544,128]{2,1,0:T(8,128)(2,1)}, u32[]{:S(2)}, u32[]{:S(2)}) collective-permute-start(bf16[4,544,128]{2,1,0:T(8,128)(2,1)} %collective-permute-done.3.refs_1_), channel_id=1, source_target_pairs={{0,4},{2,6},{4,0},{6,2},{8,12},{10,14},{12,8},{14,10},{16,20},{18,... | collective-permute-start | bytes 1671176 | tf_op jit(solution)/shard_map/ppermute | solution.py:483
  61.1 56.1 %collective-permute-start.13 = (bf16[4,544,128]{2,1,0:T(8,128)(2,1)}, bf16[4,544,128]{2,1,0:T(8,128)(2,1)}, u32[]{:S(2)}, u32[]{:S(2)}) collective-permute-start(bf16[4,544,128]{2,1,0:T(8,128)(2,1)} %collective-permute-done.1.refs_3_), channel_id=1, source_target_pairs={{0,2},{2,0},{4,6},{6,4},{8,10},{10,8},{12,14},{14,12},{16,18},{18,... | collective-permute-start | bytes 1671176 | tf_op jit(solution)/shard_map/ppermute | solution.py:483
  63.2 54.9 %collective-permute-start.12 = (bf16[4,544,128]{2,1,0:T(8,128)(2,1)}, bf16[4,544,128]{2,1,0:T(8,128)(2,1)}, u32[]{:S(2)}, u32[]{:S(2)}) collective-permute-start(bf16[4,544,128]{2,1,0:T(8,128)(2,1)} %collective-permute-done.2.refs_1_), channel_id=1, source_target_pairs={{0,2},{2,0},{4,6},{6,4},{8,10},{10,8},{12,14},{14,12},{16,18},{18,... | collective-permute-start | bytes 1671176 | tf_op jit(solution)/shard_map/ppermute | solution.py:483
  63.2 55.6 %collective-permute-start.14 = (bf16[4,544,128]{2,1,0:T(8,128)(2,1)}, bf16[4,544,128]{2,1,0:T(8,128)(2,1)}, u32[]{:S(2)}, u32[]{:S(2)}) collective-permute-start(bf16[4,544,128]{2,1,0:T(8,128)(2,1)} %collective-permute-done.4.refs_5_), channel_id=1, source_target_pairs={{0,2},{2,0},{4,6},{6,4},{8,10},{10,8},{12,14},{14,12},{16,18},{18,... | collective-permute-start | bytes 1671176 | tf_op jit(solution)/shard_map/ppermute | solution.py:483
  76.6 40.1 %collective-permute-start.15 = (f32[1,8,256]{2,1,0:T(8,128)}, f32[1,8,256]{2,1,0:T(8,128)}, u32[]{:S(2)}, u32[]{:S(2)}) collective-permute-start(f32[1,8,256]{2,1,0:T(8,128)} %loss.1.refs_12_), channel_id=1, source_target_pairs={{0,1},{1,0},{2,3},{3,2},{4,5},{5,4},{6,7},{7,6},{8,9},{9,8},{10,11... | collective-permute-start | bytes 24584 | tf_op jit(solution)/shard_map/ppermute | solution.py:503
  113.3 174.6 %collective-permute-start.5 = (bf16[4,544,128]{2,1,0:T(8,128)(2,1)}, bf16[4,544,128]{2,1,0:T(8,128)(2,1)}, u32[]{:S(2)}, u32[]{:S(2)}) collective-permute-start(bf16[4,544,128]{2,1,0:T(8,128)(2,1)} %collective-permute-done.3.refs_1_), channel_id=1, source_target_pairs={{0,2},{2,0},{4,6},{6,4},{8,10},{10,8},{12,14},{14,12},{16,18},{18,... | collective-permute-start | bytes 1671176 | tf_op jit(solution)/shard_map/ppermute | solution.py:483
  116.7 171.2 %collective-permute-start.10 = (bf16[4,544,128]{2,1,0:T(8,128)(2,1)}, bf16[4,544,128]{2,1,0:T(8,128)(2,1)}, u32[]{:S(2)}, u32[]{:S(2)}) collective-permute-start(bf16[4,544,128]{2,1,0:T(8,128)(2,1)} %collective-permute-done.6.refs_5_), channel_id=1, source_target_pairs={{0,4},{2,6},{4,0},{6,2},{8,12},{10,14},{12,8},{14,10},{16,20},{18,... | collective-permute-start | bytes 1671176 | tf_op jit(solution)/shard_map/ppermute | solution.py:483
  117.2 170.7 %collective-permute-start.11 = (bf16[4,544,128]{2,1,0:T(8,128)(2,1)}, bf16[4,544,128]{2,1,0:T(8,128)(2,1)}, u32[]{:S(2)}, u32[]{:S(2)}) collective-permute-start(bf16[4,544,128]{2,1,0:T(8,128)(2,1)} %collective-permute-done.6.refs_5_), channel_id=1, source_target_pairs={{0,6},{2,4},{4,2},{6,0},{8,14},{10,12},{12,10},{14,8},{16,22},{18,... | collective-permute-start | bytes 1671176 | tf_op jit(solution)/shard_map/ppermute | solution.py:483
  118.1 169.8 %collective-permute-start.9 = (bf16[4,544,128]{2,1,0:T(8,128)(2,1)}, bf16[4,544,128]{2,1,0:T(8,128)(2,1)}, u32[]{:S(2)}, u32[]{:S(2)}) collective-permute-start(bf16[4,544,128]{2,1,0:T(8,128)(2,1)} %collective-permute-done.6.refs_5_), channel_id=1, source_target_pairs={{0,2},{2,0},{4,6},{6,4},{8,10},{10,8},{12,14},{14,12},{16,18},{18,... | collective-permute-start | bytes 1671176 | tf_op jit(solution)/shard_map/ppermute | solution.py:483
  118.8 169.1 %collective-permute-start.8 = (bf16[4,544,128]{2,1,0:T(8,128)(2,1)}, bf16[4,544,128]{2,1,0:T(8,128)(2,1)}, u32[]{:S(2)}, u32[]{:S(2)}) collective-permute-start(bf16[4,544,128]{2,1,0:T(8,128)(2,1)} %collective-permute-done.7.refs_3_), channel_id=1, source_target_pairs={{0,2},{2,0},{4,6},{6,4},{8,10},{10,8},{12,14},{14,12},{16,18},{18,... | collective-permute-start | bytes 1671176 | tf_op jit(solution)/shard_map/ppermute | solution.py:483
